TPU v7x, 256 devices: a whole 4x4x8 slice. The times are simulated.
256 devices in a mesh: blk: 16 (over z_lo, x), rep: 16 (over y, z_hi, core).
Axes of the slice: x: 4, y: 4, z: 8 (z_hi: 2, z_lo: 4; z = z_hi * 4 + z_lo), core: 2. Of those that a mesh axis runs over, the one named last changes fastest.
Arguments:
- pixel_factors: float32 [196608, 256], P(('blk', 'rep')), may hold values from -1.5 to 1.5
- scene_factors: float32 [16384, 256], P('blk'), may hold values from -1.5 to 1.5
- elevations: bfloat16 [3, 196608, 1024], P(None, ('blk', 'rep')), may hold values from -6 to 6
- quality: bfloat16 [3, 196608, 1024], P(None, ('blk', 'rep')), may hold values from 0 to 1, as said below
- occupancy: int32 [3, 256], P(None, ('blk', 'rep')), may hold values from 0 to 1, as said below
Outputs:
- pixel_out: float32 [196608, 256], P(('blk', 'rep'))
- scene_out: float32 [16384, 256], P('blk')
Inputs may be any that keep to these rules, and one draw needn't show every extreme that they name: quality is zero on every entry of an owner's tile whose occupancy is 0; otherwise about half of the entries are nonzero. occupancy is 0 or 1 and about three quarters of the tiles are occupied.
All inputs are finite; a program needn't handle non-finite values.
Results may differ from a plain program's by a relative error of at most 0.0003.
Values sent between devices are 32-bit elements; how exact they have to be, the bound alone decides.
No kernel may reach another device: no remote copies, remote signals or barrier semaphores. Data moves between devices by JAX's collectives and lax.ppermute only.
A program may use at most 64 MiB of HBM per device.

v0:
```python
import functools

import jax
import jax.numpy as jnp
from jax import lax
from jax.experimental import pallas as pl
from jax.experimental.pallas import tpu as pltpu
from jax.sharding import PartitionSpec as P


PIX_DEV = 768
ACQ_BLK = 1024
R = 256
STEPS = 3
GROUP_ROWS = 12288
N_BLK = 16
N_Y = 4
N_ZH = 2
N_CORE = 2
N_REP = N_Y * N_ZH * N_CORE
CHUNK = 128
PAIR = 2 * CHUNK
ROW_TILE = 256
BOTH = ("blk", "rep")
ORDER = (2, 1, 3)
CALLS = (((2, 1), (3, 0)), ((0,), (2, 1), (3,)), ((0,), (2, 1), (3,)))


VMEM = pl.BlockSpec(memory_space=pltpu.VMEM)
SMEM = pl.BlockSpec(memory_space=pltpu.SMEM)
HBM = pl.BlockSpec(memory_space=pltpu.HBM)
ANY = pl.BlockSpec(memory_space=pl.ANY)

F32, BF16 = jnp.float32, jnp.bfloat16
PIXELS = jax.ShapeDtypeStruct((PIX_DEV, R), F32)
HALF = jax.ShapeDtypeStruct((PIX_DEV, R), BF16)
TURNED = jax.ShapeDtypeStruct((R, PIX_DEV), BF16)
PIECE = jax.ShapeDtypeStruct((R, CHUNK), F32)
ROWS = jax.ShapeDtypeStruct((CHUNK, R), F32)
TOKEN = jax.ShapeDtypeStruct((8, 128), F32)
FLOPS = 3 * 2 * PIX_DEV * ACQ_BLK * R


def moved(value, blk=0, y=0, zh=0, core=0):
    pairs = []
    for b in range(N_BLK):
        for r in range(N_REP):
            ry, rz, rc = r // (N_ZH * N_CORE), (r // N_CORE) % N_ZH, r % N_CORE
            db = (b + blk) % N_BLK
            dr = (((ry + y) % N_Y) * N_ZH + (rz + zh) % N_ZH) * N_CORE + (rc + core) % N_CORE
            pairs.append((b * N_REP + r, db * N_REP + dr))
    return lax.ppermute(value, BOTH, pairs)


def position():
    rep = lax.axis_index("rep")
    return lax.rem(rep, N_CORE), lax.div(rep, N_ZH * N_CORE)


def split(value):
    high = value.astype(BF16)
    low = (value - high.astype(F32)).astype(BF16)
    return high, low


NN = (((1,), (0,)), ((), ()))
NT = (((1,), (1,)), ((), ()))


def dot3(a_high, a_low, b_high, b_low, dims):
    dot = functools.partial(lax.dot_general, dimension_numbers=dims, preferred_element_type=F32)
    return dot(a_high, b_high) + (dot(a_high, b_low) + dot(a_low, b_high))


def call(kernel, out, in_specs, out_specs, args, mib=4, flops=0, scratch=()):
    return pl.pallas_call(
        kernel,
        out_shape=out,
        in_specs=in_specs,
        out_specs=out_specs,
        scratch_shapes=list(scratch),
        compiler_params=pltpu.CompilerParams(vmem_limit_bytes=mib << 20),
        cost_estimate=pl.CostEstimate(flops=flops, bytes_accessed=1 << 20, transcendentals=0),
    )(*args)


def prepare_kernel(pixels, scene, uh, ul, uth, utl, vh, vl, own):
    core, y = position()
    for r in range(N_Y):
        at = lax.rem(y + r, N_Y) * PAIR
        vh[r], vl[r] = split(scene[pl.ds(pl.multiple_of(at, PAIR), PAIR), :].T)
    own[...] = scene[pl.ds(pl.multiple_of(y * PAIR + core * CHUNK, CHUNK), CHUNK), :].T
    for t in range(PIX_DEV // ROW_TILE):
        rows = pl.ds(t * ROW_TILE, ROW_TILE)
        value = pixels[rows, :]
        uh[rows, :], ul[rows, :] = split(value)
        uth[:, rows], utl[:, rows] = split(value.T)


def prepare(pixels, scene):
    blocks = jax.ShapeDtypeStruct((N_Y, R, PAIR), BF16)
    out = [HALF, HALF, TURNED, TURNED, blocks, blocks, PIECE]
    res = call(prepare_kernel, out, [VMEM] * 2, [VMEM] * len(out), (pixels, scene))
    return res[:4], res[4:6], res[6]


def misfit_kernel(step, chunks, carried, occupancy, uh, ul, uth, utl, tile, weight, *refs):
    core, y = position()
    count = len(chunks)
    if step:
        mine, other, refs = refs[:count], refs[count : 2 * count], refs[2 * count :]
        refs, (vh, vl) = refs[:-2], refs[-2:]
        for k in range(count):
            first = jnp.where(core == 0, mine[k][...], other[k][...])
            second = jnp.where(core == 0, other[k][...], mine[k][...])
            vh[k], vl[k] = split(jnp.concatenate([first, second], axis=1))
    else:
        (vh, vl), refs = refs[:2], refs[2:]
    sent, kept, mh, ml = refs[-4:]
    if carried:
        sent[count] = refs[0][0]
    flag = occupancy[step, 0].astype(F32)

    def one(k, r, at):
        columns = pl.ds(pl.multiple_of(lax.rem(y + r, N_Y) * PAIR, PAIR), PAIR)
        v_high, v_low = vh[at], vl[at]
        predicted = dot3(uh[...], ul[...], v_high, v_low, NN)
        misfit = (weight[:, columns].astype(F32) * flag) * (tile[:, columns].astype(F32) - predicted)
        m_high, m_low = split(misfit)
        mh[k] = m_high
        ml[k] = m_low
        grad = dot3(uth[...], utl[...], m_high, m_low, NN)
        left, right = grad[:, :CHUNK], grad[:, CHUNK:]
        kept[k] = jnp.where(core == 0, left, right)
        sent[k] = jnp.where(core == 0, right, left)

    if count == 1:
        one(0, chunks[0], 0 if step else chunks[0])
    else:

        @pl.loop(0, count)
        def _(k):
            r = chunks[0] + k * (chunks[1] - chunks[0])
            one(k, r, k if step else r)


def misfit_part(step, chunks, occupancy, factors, tiles, block, carried, before):
    count = len(chunks)
    pieces = lambda n: jax.ShapeDtypeStruct((n, R, CHUNK), F32)
    misfits = jax.ShapeDtypeStruct((count, PIX_DEV, PAIR), BF16)
    blocks = jax.ShapeDtypeStruct((count, R, PAIR), BF16)
    out = [pieces(count + len(carried)), pieces(count), misfits, misfits] + ([blocks] * 2 if step else [])
    ins = [occupancy, *factors, *tiles, *block, *carried]
    return call(
        functools.partial(misfit_kernel, step, chunks, len(carried)),
        out,
        [SMEM] + [VMEM] * (len(ins) - 1) + [ANY] * len(before),
        [VMEM] * len(out),
        (*ins, *before),
        mib=6,
        flops=FLOPS * count // 2,
    )


def pixel_kernel(step, pixels, *refs):
    last = step + 1 == STEPS
    calls = len(CALLS[step])
    rows_of = [(n, k) for n, chunks in enumerate(CALLS[step]) for k in range(len(chunks))]
    mh, ml, refs = refs[:calls], refs[calls : 2 * calls], refs[2 * calls :]
    if step:
        vh, vl, refs = refs[:calls], refs[calls : 2 * calls], refs[2 * calls :]
    else:
        vh, vl, refs = refs[0], refs[1], refs[2:]
    outs = refs[1:]
    outs[0][...] = jnp.zeros_like(outs[0])

    @pl.loop(0, PIX_DEV // ROW_TILE)
    def _(t):
        rows = pl.ds(pl.multiple_of(t * ROW_TILE, ROW_TILE), ROW_TILE)
        grad = jnp.zeros((ROW_TILE, R), F32)
        for n, k in rows_of:
            r = CALLS[step][n][k]
            v_high, v_low = (vh[n][k], vl[n][k]) if step else (vh[r], vl[r])
            grad = grad + dot3(mh[n][k, rows, :], ml[n][k, rows, :], v_high, v_low, NT)
        value = pixels[rows, :] + (8.0 / ACQ_BLK) * grad
        outs[1][rows, :] = value
        if not last:
            outs[2][rows, :], outs[3][rows, :] = split(value)
            outs[4][:, rows], outs[5][:, rows] = split(value.T)


def pixel_step(step, pixels, parts, blocks, after):
    last = step + 1 == STEPS
    ins = [pixels, *(p[2] for p in parts), *(p[3] for p in parts), *blocks, after]
    out = [TOKEN, PIXELS]
    if not last:
        out += [HALF, HALF, TURNED, TURNED]
    res = call(
        functools.partial(pixel_kernel, step),
        out,
        [VMEM] * (len(ins) - 1) + [ANY],
        [VMEM] * len(out),
        ins,
        flops=FLOPS,
    )
    return res[0], res[1], res[2:]


def add_kernel(*refs):
    kept, swapped, first, second = refs[:-3], *refs[-3:]
    first[...] = kept[0][0] + swapped[0]
    second[...] = kept[-1][-1 % kept[-1].shape[0]] + swapped[1]


def add_pair(kept, swapped):
    return call(add_kernel, [PIECE] * 2, [VMEM] * (len(kept) + 1), [VMEM] * 2, (*kept, swapped))


def total_kernel(own, summed, first, second, third, out):
    total = summed[...] + (first[...] + (second[...] + third[...]))
    out[...] = 0.5 * own[...] + (8.0 / GROUP_ROWS) * total


def fresh_kernel(last, a, b, after, out):
    value = a[...] + b[...]
    out[...] = value.T if last else value


def join_kernel(*refs):
    for r in range(N_Y):
        refs[-1][r] = refs[r][...]


def assemble_kernel(mine, other, out, sems):
    core, y = position()
    copies = []
    for r in range(N_Y):
        for k, pieces in enumerate((mine, other)):
            at = lax.rem(y + r, N_Y) * PAIR + lax.rem(core + k, N_CORE) * CHUNK
            rows = pl.ds(pl.multiple_of(at, CHUNK), CHUNK)
            copies.append(pltpu.make_async_copy(pieces.at[r], out.at[rows, :], sems.at[k, r]))
    for c in copies:
        c.start()
    for c in copies:
        c.wait()


def steps(pixel_factors, scene_factors, elevations, quality, occupancy):
    pixels = pixel_factors
    factors, blocks, own = prepare(pixel_factors, scene_factors)
    tiles = elevations[0], quality[0]
    mine = other = None
    for step in range(STEPS):
        last = step + 1 == STEPS
        parts = []
        for n, chunks in enumerate(CALLS[step]):
            block = [mine[r] for r in chunks] + [other[r] for r in chunks] if step else blocks
            carried = [parts[0][0]] if step and n == 2 else []
            before = [parts[-1][1]] if parts else []
            parts.append(misfit_part(step, chunks, occupancy, factors, tiles, block, carried, before))
        if step:
            blocks = [p[4] for p in parts] + [p[5] for p in parts]
        kept = [p[1] for p in parts]
        early = moved(parts[-2][0], core=1)
        late = moved(parts[-1][0], core=1)
        sums = add_pair(kept[-2:-1], early)
        arrived = [moved(v, y=r) for r, v in zip(ORDER, sums)]
        sums = add_pair([kept[-1], kept[0]] if step else kept[-1:], late)
        arrived.append(moved(sums[0], y=ORDER[2]))
        half = call(total_kernel, PIECE, [VMEM] * 5, VMEM, (own, sums[1], *arrived))
        go = STEPS - 1 if last else -1
        far, near = moved(half, blk=go, zh=1), moved(half, blk=go)
        token, pixels, factors = pixel_step(step, pixels, parts, blocks, half)
        if not last:
            elevations, quality, token = lax.optimization_barrier((elevations, quality, token))
            tiles = elevations[step + 1], quality[step + 1]
        own = call(
            functools.partial(fresh_kernel, last),
            ROWS if last else PIECE,
            [VMEM] * 2 + [ANY],
            VMEM,
            (near, far, token),
        )
        mine, other = {0: own}, {}
        if not last:
            other[0] = moved(own, core=1)
        for r in ORDER:
            mine[r] = moved(own, y=-r)
        if not last:
            for r in ORDER:
                other[r] = moved(mine[r], core=1)
    joined = jax.ShapeDtypeStruct((N_Y, CHUNK, R), F32)
    joined = call(join_kernel, joined, [VMEM] * N_Y, VMEM, [mine[r] for r in range(N_Y)])
    scene = call(
        assemble_kernel,
        jax.ShapeDtypeStruct((ACQ_BLK, R), F32),
        [VMEM] * 2,
        HBM,
        (joined, moved(joined, core=1)),
        scratch=[pltpu.SemaphoreType.DMA((N_CORE, N_Y))],
    )
    return (pixels, scene)


def solution(mesh):
    in_specs = (
        P(("blk", "rep"), None),
        P("blk", None),
        P(None, ("blk", "rep"), None),
        P(None, ("blk", "rep"), None),
        P(None, ("blk", "rep")),
    )
    out_specs = (P(("blk", "rep"), None), P("blk", None))
    return jax.shard_map(steps, mesh=mesh, in_specs=in_specs, out_specs=out_specs, check_vma=False)
```

profile of v0, /device:TPU:2, one launch (start us, length us, event | category | flops | bytes accessed | tf_op | source)
XLA Modules:
  0.0 140.6 jit_solution(11869399277774467048)
XLA Ops:
  4.3 2.5 %slice_bitcast_fusion.4 = (bf16[768,1024]{1,0:T(8,128)(2,1)S(1)}, bf16[768,1024]{1,0:T(8,128)(2,1)S(1)}) fusion(bf16[3,768,1024]{2,1,0:T(8,128)(2,1)} %param.8, bf16[3,768,1024]{2,1,0:T(8,128)(2,1)} %param.7), kind=kLoop, calls=%fused_computation.4 | loop fusion | bytes 6291456 | tf_op jit(solution)/shard_map/squeeze | solution.py:251
  6.8 3.4 %shard_map.69 = (f32[2,256,128]{2,1,0:T(8,128)S(1)}, f32[2,256,128]{2,1,0:T(8,128)S(1)}, bf16[2,768,256]{2,1,0:T(8,128)(2,1)S(1)}, bf16[2,768,256]{2,1,0:T(8,128)(2,1)S(1)}) custom-call(s32[3,1]{1,0:T(4,128)S(1)} %copy.7.occupancy, bf16[768,256]{1,0:T(8,128)(2,1)S(1)} %get-tuple-element.85.uh, bf16[768,256]{1,0:T(8,128)(2,1)S(1)} %get-tuple-element.86.ul, ...), custom_call_target="tpu_custom_call" | custom-call | flops 1207959552 | bytes 1048576 | tf_op jit(solution)/shard_map/pallas_call | solution.py:76
  10.3 3.4 %shard_map.70 = (f32[2,256,128]{2,1,0:T(8,128)S(1)}, f32[2,256,128]{2,1,0:T(8,128)S(1)}, bf16[2,768,256]{2,1,0:T(8,128)(2,1)S(1)}, bf16[2,768,256]{2,1,0:T(8,128)(2,1)S(1)}) custom-call(s32[3,1]{1,0:T(4,128)S(1)} %copy.7.occupancy, bf16[768,256]{1,0:T(8,128)(2,1)S(1)} %get-tuple-element.85.uh, bf16[768,256]{1,0:T(8,128)(2,1)S(1)} %get-tuple-element.86.ul, ...), custom_call_target="tpu_custom_call" | custom-call | flops 1207959552 | bytes 1048576 | tf_op jit(solution)/shard_map/pallas_call | solution.py:76
  14.3 3.3 %collective-permute-start.2 = (f32[256,128]{1,0:T(8,128)S(1)}, f32[256,128]{1,0:T(8,128)S(1)}, u32[]{:S(2)}, u32[]{:S(2)}) collective-permute-start(f32[256,128]{1,0:T(8,128)S(1)} %get-tuple-element.101), channel_id=1, source_target_pairs={{0,8},{1,9},{2,10},{3,11},{4,12},{5,13},{6,14},{7,15},{8,0},{9,1},... | collective-permute-start | bytes 393224 | tf_op jit(solution)/shard_map/ppermute | solution.py:52
  18.3 2.6 %collective-permute-start.4 = (f32[256,128]{1,0:T(8,128)S(1)}, f32[256,128]{1,0:T(8,128)S(1)}, u32[]{:S(2)}, u32[]{:S(2)}) collective-permute-start(f32[256,128]{1,0:T(8,128)S(1)} %get-tuple-element.103), channel_id=1, source_target_pairs={{0,12},{1,13},{2,14},{3,15},{4,0},{5,1},{6,2},{7,3},{8,4},{9,5},{1... | collective-permute-start | bytes 393224 | tf_op jit(solution)/shard_map/ppermute | solution.py:52
  22.2 2.3 %collective-permute-done.3.second = f32[256,128]{1,0:T(8,128)S(1)} collective-permute-done((f32[256,128]{1,0:T(8,128)S(1)}, f32[256,128]{1,0:T(8,128)S(1)}, u32[]{:S(2)}, u32[]{:S(2)}) %collective-permute-start.3) | collective-permute-done | bytes 131104 | tf_op jit(solution)/shard_map/ppermute | solution.py:52
  24.5 7.2 %collective-permute-start.6 = (f32[256,128]{1,0:T(8,128)S(1)}, f32[256,128]{1,0:T(8,128)S(1)}, u32[]{:S(2)}, u32[]{:S(2)}) collective-permute-start(f32[256,128]{1,0:T(8,128)S(1)} %shard_map.73.refs_6_), channel_id=1, source_target_pairs={{0,242},{1,243},{2,240},{3,241},{4,246},{5,247},{6,244},{7,245},{8... | collective-permute-start | bytes 393224 | tf_op jit(solution)/shard_map/ppermute | solution.py:52
  33.2 2.0 %shard_map.74 = (f32[8,128]{1,0:T(8,128)S(1)}, f32[768,256]{1,0:T(8,128)S(1)}, bf16[768,256]{1,0:T(8,128)(2,1)S(1)}, bf16[768,256]{1,0:T(8,128)(2,1)S(1)}, bf16[...) custom-call(f32[768,256]{1,0:T(8,128)S(1)} %copy-done.1, bf16[2,768,256]{2,1,0:T(8,128)(2,1)S(1)} %get-tuple-element.91.refs_0_, ...), custom_call_target="tpu_custom_call" | custom-call | flops 1207959552 | bytes 1048576 | tf_op jit(solution)/shard_map/pallas_call | solution.py:76
  36.0 2.7 %collective-permute-done.5.a = f32[256,128]{1,0:T(8,128)S(1)} collective-permute-done((f32[256,128]{1,0:T(8,128)S(1)}, f32[256,128]{1,0:T(8,128)S(1)}, u32[]{:S(2)}, u32[]{:S(2)}) %collective-permute-start.5) | collective-permute-done | bytes 131104 | tf_op jit(solution)/shard_map/ppermute | solution.py:52
  38.8 2.8 %collective-permute-start.9 = (f32[256,128]{1,0:T(8,128)S(1)}, f32[256,128]{1,0:T(8,128)S(1)}, u32[]{:S(2)}, u32[]{:S(2)}) collective-permute-start(f32[256,128]{1,0:T(8,128)S(1)} %shard_map.75.refs_0_.own), channel_id=1, source_target_pairs={{0,12},{1,13},{2,14},{3,15},{4,0},{5,1},{6,2},{7,3},{8,4},{9,5},{1... | collective-permute-start | bytes 393224 | tf_op jit(solution)/shard_map/ppermute | solution.py:52
  43.0 4.4 %collective-permute-done.9.refs_1_ = f32[256,128]{1,0:T(8,128)S(1)} collective-permute-done((f32[256,128]{1,0:T(8,128)S(1)}, f32[256,128]{1,0:T(8,128)S(1)}, u32[]{:S(2)}, u32[]{:S(2)}) %collective-permute-start.9) | collective-permute-done | bytes 131104 | tf_op jit(solution)/shard_map/ppermute | solution.py:52
  47.4 2.1 %collective-permute-done.8.refs_0_ = f32[256,128]{1,0:T(8,128)S(1)} collective-permute-done((f32[256,128]{1,0:T(8,128)S(1)}, f32[256,128]{1,0:T(8,128)S(1)}, u32[]{:S(2)}, u32[]{:S(2)}) %collective-permute-start.8) | collective-permute-done | bytes 131104 | tf_op jit(solution)/shard_map/ppermute | solution.py:52
  53.1 3.5 %shard_map.77 = (f32[2,256,128]{2,1,0:T(8,128)S(1)}, f32[2,256,128]{2,1,0:T(8,128)S(1)}, bf16[2,768,256]{2,1,0:T(8,128)(2,1)S(1)}, bf16[2,768,256]{2,1,0:T(8,128...) custom-call(s32[3,1]{1,0:T(4,128)S(1)} %copy.7.occupancy, ...), custom_call_target="tpu_custom_call" | custom-call | flops 1207959552 | bytes 1048576 | tf_op jit(solution)/shard_map/pallas_call | solution.py:76
  61.2 2.6 %collective-permute-start.18 = (f32[256,128]{1,0:T(8,128)S(1)}, f32[256,128]{1,0:T(8,128)S(1)}, u32[]{:S(2)}, u32[]{:S(2)}) collective-permute-start(f32[256,128]{1,0:T(8,128)S(1)} %get-tuple-element.134), channel_id=1, source_target_pairs={{0,12},{1,13},{2,14},{3,15},{4,0},{5,1},{6,2},{7,3},{8,4},{9,5},{1... | collective-permute-start | bytes 393224 | tf_op jit(solution)/shard_map/ppermute | solution.py:52
  63.8 3.5 %collective-permute-done.16.first = f32[256,128]{1,0:T(8,128)S(1)} collective-permute-done((f32[256,128]{1,0:T(8,128)S(1)}, f32[256,128]{1,0:T(8,128)S(1)}, u32[]{:S(2)}, u32[]{:S(2)}) %collective-permute-start.16) | collective-permute-done | bytes 131104 | tf_op jit(solution)/shard_map/ppermute | solution.py:52
  67.3 2.3 %collective-permute-done.17.second = f32[256,128]{1,0:T(8,128)S(1)} collective-permute-done((f32[256,128]{1,0:T(8,128)S(1)}, f32[256,128]{1,0:T(8,128)S(1)}, u32[]{:S(2)}, u32[]{:S(2)}) %collective-permute-start.17) | collective-permute-done | bytes 131104 | tf_op jit(solution)/shard_map/ppermute | solution.py:52
  69.6 3.6 %collective-permute-start.20 = (f32[256,128]{1,0:T(8,128)S(1)}, f32[256,128]{1,0:T(8,128)S(1)}, u32[]{:S(2)}, u32[]{:S(2)}) collective-permute-start(f32[256,128]{1,0:T(8,128)S(1)} %shard_map.81.refs_12_), channel_id=1, source_target_pairs={{0,242},{1,243},{2,240},{3,241},{4,246},{5,247},{6,244},{7,245},{8... | collective-permute-start | bytes 393224 | tf_op jit(solution)/shard_map/ppermute | solution.py:52
  74.8 2.1 %shard_map.82 = (f32[8,128]{1,0:T(8,128)S(1)}, f32[768,256]{1,0:T(8,128)S(1)}, bf16[768,256]{1,0:T(8,128)(2,1)S(1)}, bf16[768,256]{1,0:T(8,128)(2,1)S(1)}, bf16[...) custom-call(f32[768,256]{1,0:T(8,128)S(1)} %get-tuple-element.104.pixels, ...), custom_call_target="tpu_custom_call" | custom-call | flops 1207959552 | bytes 1048576 | tf_op jit(solution)/shard_map/pallas_call | solution.py:76
  76.8 3.2 %collective-permute-done.20.b = f32[256,128]{1,0:T(8,128)S(1)} collective-permute-done((f32[256,128]{1,0:T(8,128)S(1)}, f32[256,128]{1,0:T(8,128)S(1)}, u32[]{:S(2)}, u32[]{:S(2)}) %collective-permute-start.20) | collective-permute-done | bytes 131104 | tf_op jit(solution)/shard_map/ppermute | solution.py:52
  83.8 2.5 %collective-permute-done.23.refs_1_ = f32[256,128]{1,0:T(8,128)S(1)} collective-permute-done((f32[256,128]{1,0:T(8,128)S(1)}, f32[256,128]{1,0:T(8,128)S(1)}, u32[]{:S(2)}, u32[]{:S(2)}) %collective-permute-start.23) | collective-permute-done | bytes 131104 | tf_op jit(solution)/shard_map/ppermute | solution.py:52
  86.3 2.2 %collective-permute-done.22.refs_0_ = f32[256,128]{1,0:T(8,128)S(1)} collective-permute-done((f32[256,128]{1,0:T(8,128)S(1)}, f32[256,128]{1,0:T(8,128)S(1)}, u32[]{:S(2)}, u32[]{:S(2)}) %collective-permute-start.22) | collective-permute-done | bytes 131104 | tf_op jit(solution)/shard_map/ppermute | solution.py:52
  91.8 3.5 %shard_map.85 = (f32[2,256,128]{2,1,0:T(8,128)S(1)}, f32[2,256,128]{2,1,0:T(8,128)S(1)}, bf16[2,768,256]{2,1,0:T(8,128)(2,1)S(1)}, bf16[2,768,256]{2,1,0:T(8,128...) custom-call(s32[3,1]{1,0:T(4,128)S(1)} %copy.7.occupancy, ...), custom_call_target="tpu_custom_call" | custom-call | flops 1207959552 | bytes 1048576 | tf_op jit(solution)/shard_map/pallas_call | solution.py:76
  95.9 2.0 %shard_map.86 = (f32[2,256,128]{2,1,0:T(8,128)S(1)}, f32[1,256,128]{2,1,0:T(8,128)S(1)}, bf16[1,768,256]{2,1,0:T(8,128)(2,1)S(1)}, bf16[1,768,256]{2,1,0:T(8,128...) custom-call(s32[3,1]{1,0:T(4,128)S(1)} %copy.7.occupancy, ...), custom_call_target="tpu_custom_call" | custom-call | flops 603979776 | bytes 1048576 | tf_op jit(solution)/shard_map/pallas_call | solution.py:76
  102.2 3.8 %collective-permute-done.30.first = f32[256,128]{1,0:T(8,128)S(1)} collective-permute-done((f32[256,128]{1,0:T(8,128)S(1)}, f32[256,128]{1,0:T(8,128)S(1)}, u32[]{:S(2)}, u32[]{:S(2)}) %collective-permute-start.30) | collective-permute-done | bytes 131104 | tf_op jit(solution)/shard_map/ppermute | solution.py:52
  106.0 2.3 %collective-permute-done.31.second = f32[256,128]{1,0:T(8,128)S(1)} collective-permute-done((f32[256,128]{1,0:T(8,128)S(1)}, f32[256,128]{1,0:T(8,128)S(1)}, u32[]{:S(2)}, u32[]{:S(2)}) %collective-permute-start.31) | collective-permute-done | bytes 131104 | tf_op jit(solution)/shard_map/ppermute | solution.py:52
  108.3 5.8 %collective-permute-start.34 = (f32[256,128]{1,0:T(8,128)S(1)}, f32[256,128]{1,0:T(8,128)S(1)}, u32[]{:S(2)}, u32[]{:S(2)}) collective-permute-start(f32[256,128]{1,0:T(8,128)S(1)} %shard_map.89.refs_12_), channel_id=1, source_target_pairs={{0,34},{1,35},{2,32},{3,33},{4,38},{5,39},{6,36},{7,37},{8,42},{9,... | collective-permute-start | bytes 393224 | tf_op jit(solution)/shard_map/ppermute | solution.py:52
  114.1 2.9 %collective-permute-start.33 = (f32[256,128]{1,0:T(8,128)S(1)}, f32[256,128]{1,0:T(8,128)S(1)}, u32[]{:S(2)}, u32[]{:S(2)}) collective-permute-start(f32[256,128]{1,0:T(8,128)S(1)} %shard_map.89.refs_12_), channel_id=1, source_target_pairs={{0,32},{1,33},{2,34},{3,35},{4,36},{5,37},{6,38},{7,39},{8,40},{9,... | collective-permute-start | bytes 393224 | tf_op jit(solution)/shard_map/ppermute | solution.py:52
  117.0 2.7 %shard_map.90 = (f32[8,128]{1,0:T(8,128)S(1)}, f32[768,256]{1,0:T(8,128)}) custom-call(f32[768,256]{1,0:T(8,128)S(1)} %get-tuple-element.135.pixels, bf16[1,768,256]{2,1,0:T(8,128)(2,1)S(1)} %get-tuple-element.144.refs_0_, bf16[2,768,256]{2,1,0:T(8,128)(2,1)S(1)} %get-tuple-element.146.refs_1_, bf16[1,768,256]{2,1,0:T(8,128)(2,1)S(1)} %get-tuple-element.149.refs_2_, ...), custom_call_target="tpu_custom_call" | custom-call | flops 1207959552 | bytes 1048576 | tf_op jit(solution)/shard_map/pallas_call | solution.py:76
  119.7 4.2 %collective-permute-done.34.b = f32[256,128]{1,0:T(8,128)S(1)} collective-permute-done((f32[256,128]{1,0:T(8,128)S(1)}, f32[256,128]{1,0:T(8,128)S(1)}, u32[]{:S(2)}, u32[]{:S(2)}) %collective-permute-start.34) | collective-permute-done | bytes 131104 | tf_op jit(solution)/shard_map/ppermute | solution.py:52
  123.9 3.2 %collective-permute-done.33.a = f32[256,128]{1,0:T(8,128)S(1)} collective-permute-done((f32[256,128]{1,0:T(8,128)S(1)}, f32[256,128]{1,0:T(8,128)S(1)}, u32[]{:S(2)}, u32[]{:S(2)}) %collective-permute-start.33) | collective-permute-done | bytes 131104 | tf_op jit(solution)/shard_map/ppermute | solution.py:52
  127.3 2.3 %collective-permute-start.36 = (f32[128,256]{1,0:T(8,128)S(1)}, f32[128,256]{1,0:T(8,128)S(1)}, u32[]{:S(2)}, u32[]{:S(2)}) collective-permute-start(f32[128,256]{1,0:T(8,128)S(1)} %shard_map.91.refs_0_), channel_id=1, source_target_pairs={{0,8},{1,9},{2,10},{3,11},{4,12},{5,13},{6,14},{7,15},{8,0},{9,1},... | collective-permute-start | bytes 393224 | tf_op jit(solution)/shard_map/ppermute | solution.py:52
  131.3 5.4 %collective-permute-done.37.refs_3_ = f32[128,256]{1,0:T(8,128)S(1)} collective-permute-done((f32[128,256]{1,0:T(8,128)S(1)}, f32[128,256]{1,0:T(8,128)S(1)}, u32[]{:S(2)}, u32[]{:S(2)}) %collective-permute-start.37) | collective-permute-done | bytes 131104 | tf_op jit(solution)/shard_map/ppermute | solution.py:52
  (94 shorter events, 37.3 us)
Async XLA Ops:
  10.2 4.1 %collective-permute-start.1 = (f32[2,256,128]{2,1,0:T(8,128)S(1)}, f32[2,256,128]{2,1,0:T(8,128)S(1)}, u32[]{:S(2)}, u32[]{:S(2)}) collective-permute-start(f32[2,256,128]{2,1,0:T(8,128)S(1)} %get-tuple-element.100), channel_id=1, source_target_pairs={{0,1},{1,0},{2,3},{3,2},{4,5},{5,4},{6,7},{7,6},{8,9},{9,8},{10,11... | collective-permute-start | bytes 786440 | tf_op jit(solution)/shard_map/ppermute | solution.py:52
  13.7 4.6 %collective-permute-start = (f32[2,256,128]{2,1,0:T(8,128)S(1)}, f32[2,256,128]{2,1,0:T(8,128)S(1)}, u32[]{:S(2)}, u32[]{:S(2)}) collective-permute-start(f32[2,256,128]{2,1,0:T(8,128)S(1)} %get-tuple-element.98), channel_id=1, source_target_pairs={{0,1},{1,0},{2,3},{3,2},{4,5},{5,4},{6,7},{7,6},{8,9},{9,8},{10,11... | collective-permute-start | bytes 786440 | tf_op jit(solution)/shard_map/ppermute | solution.py:52
  14.3 7.9 %collective-permute-start.2 = (f32[256,128]{1,0:T(8,128)S(1)}, f32[256,128]{1,0:T(8,128)S(1)}, u32[]{:S(2)}, u32[]{:S(2)}) collective-permute-start(f32[256,128]{1,0:T(8,128)S(1)} %get-tuple-element.101), channel_id=1, source_target_pairs={{0,8},{1,9},{2,10},{3,11},{4,12},{5,13},{6,14},{7,15},{8,0},{9,1},... | collective-permute-start | bytes 393224 | tf_op jit(solution)/shard_map/ppermute | solution.py:52
  17.6 6.9 %collective-permute-start.3 = (f32[256,128]{1,0:T(8,128)S(1)}, f32[256,128]{1,0:T(8,128)S(1)}, u32[]{:S(2)}, u32[]{:S(2)}) collective-permute-start(f32[256,128]{1,0:T(8,128)S(1)} %get-tuple-element.102), channel_id=1, source_target_pairs={{0,4},{1,5},{2,6},{3,7},{4,8},{5,9},{6,10},{7,11},{8,12},{9,13},{1... | collective-permute-start | bytes 393224 | tf_op jit(solution)/shard_map/ppermute | solution.py:52
  18.3 6.2 %collective-permute-start.4 = (f32[256,128]{1,0:T(8,128)S(1)}, f32[256,128]{1,0:T(8,128)S(1)}, u32[]{:S(2)}, u32[]{:S(2)}) collective-permute-start(f32[256,128]{1,0:T(8,128)S(1)} %get-tuple-element.103), channel_id=1, source_target_pairs={{0,12},{1,13},{2,14},{3,15},{4,0},{5,1},{6,2},{7,3},{8,4},{9,5},{1... | collective-permute-start | bytes 393224 | tf_op jit(solution)/shard_map/ppermute | solution.py:52
  24.5 11.5 %collective-permute-start.6 = (f32[256,128]{1,0:T(8,128)S(1)}, f32[256,128]{1,0:T(8,128)S(1)}, u32[]{:S(2)}, u32[]{:S(2)}) collective-permute-start(f32[256,128]{1,0:T(8,128)S(1)} %shard_map.73.refs_6_), channel_id=1, source_target_pairs={{0,242},{1,243},{2,240},{3,241},{4,246},{5,247},{6,244},{7,245},{8... | collective-permute-start | bytes 393224 | tf_op jit(solution)/shard_map/ppermute | solution.py:52
  31.8 7.0 %collective-permute-start.5 = (f32[256,128]{1,0:T(8,128)S(1)}, f32[256,128]{1,0:T(8,128)S(1)}, u32[]{:S(2)}, u32[]{:S(2)}) collective-permute-start(f32[256,128]{1,0:T(8,128)S(1)} %shard_map.73.refs_6_), channel_id=1, source_target_pairs={{0,240},{1,241},{2,242},{3,243},{4,244},{5,245},{6,246},{7,247},{8... | collective-permute-start | bytes 393224 | tf_op jit(solution)/shard_map/ppermute | solution.py:52
  38.8 8.6 %collective-permute-start.9 = (f32[256,128]{1,0:T(8,128)S(1)}, f32[256,128]{1,0:T(8,128)S(1)}, u32[]{:S(2)}, u32[]{:S(2)}) collective-permute-start(f32[256,128]{1,0:T(8,128)S(1)} %shard_map.75.refs_0_.own), channel_id=1, source_target_pairs={{0,12},{1,13},{2,14},{3,15},{4,0},{5,1},{6,2},{7,3},{8,4},{9,5},{1... | collective-permute-start | bytes 393224 | tf_op jit(solution)/shard_map/ppermute | solution.py:52
  41.6 7.9 %collective-permute-start.8 = (f32[256,128]{1,0:T(8,128)S(1)}, f32[256,128]{1,0:T(8,128)S(1)}, u32[]{:S(2)}, u32[]{:S(2)}) collective-permute-start(f32[256,128]{1,0:T(8,128)S(1)} %shard_map.75.refs_0_.own), channel_id=1, source_target_pairs={{0,8},{1,9},{2,10},{3,11},{4,12},{5,13},{6,14},{7,15},{8,0},{9,1},... | collective-permute-start | bytes 393224 | tf_op jit(solution)/shard_map/ppermute | solution.py:52
  42.8 8.2 %collective-permute-start.12 = (f32[256,128]{1,0:T(8,128)S(1)}, f32[256,128]{1,0:T(8,128)S(1)}, u32[]{:S(2)}, u32[]{:S(2)}) collective-permute-start(f32[256,128]{1,0:T(8,128)S(1)} %shard_map.75.refs_0_.own), channel_id=1, source_target_pairs={{0,4},{1,5},{2,6},{3,7},{4,8},{5,9},{6,10},{7,11},{8,12},{9,13},{1... | collective-permute-start | bytes 393224 | tf_op jit(solution)/shard_map/ppermute | solution.py:52
  42.9 8.1 %collective-permute-start.7 = (f32[256,128]{1,0:T(8,128)S(1)}, f32[256,128]{1,0:T(8,128)S(1)}, u32[]{:S(2)}, u32[]{:S(2)}) collective-permute-start(f32[256,128]{1,0:T(8,128)S(1)} %shard_map.75.refs_0_.own), channel_id=1, source_target_pairs={{0,1},{1,0},{2,3},{3,2},{4,5},{5,4},{6,7},{7,6},{8,9},{9,8},{10,11... | collective-permute-start | bytes 393224 | tf_op jit(solution)/shard_map/ppermute | solution.py:52
  47.4 5.7 %collective-permute-start.11 = (f32[256,128]{1,0:T(8,128)S(1)}, f32[256,128]{1,0:T(8,128)S(1)}, u32[]{:S(2)}, u32[]{:S(2)}) collective-permute-start(f32[256,128]{1,0:T(8,128)S(1)} %collective-permute-done.9.refs_1_), channel_id=1, source_target_pairs={{0,1},{1,0},{2,3},{3,2},{4,5},{5,4},{6,7},{7,6},{8,9},{9,8},{10,11... | collective-permute-start | bytes 393224 | tf_op jit(solution)/shard_map/ppermute | solution.py:52
  51.0 6.1 %collective-permute-start.13 = (f32[256,128]{1,0:T(8,128)S(1)}, f32[256,128]{1,0:T(8,128)S(1)}, u32[]{:S(2)}, u32[]{:S(2)}) collective-permute-start(f32[256,128]{1,0:T(8,128)S(1)} %collective-permute-done.12.refs_0_), channel_id=1, source_target_pairs={{0,1},{1,0},{2,3},{3,2},{4,5},{5,4},{6,7},{7,6},{8,9},{9,8},{10,11... | collective-permute-start | bytes 393224 | tf_op jit(solution)/shard_map/ppermute | solution.py:52
  59.3 8.0 %collective-permute-start.16 = (f32[256,128]{1,0:T(8,128)S(1)}, f32[256,128]{1,0:T(8,128)S(1)}, u32[]{:S(2)}, u32[]{:S(2)}) collective-permute-start(f32[256,128]{1,0:T(8,128)S(1)} %get-tuple-element.132), channel_id=1, source_target_pairs={{0,8},{1,9},{2,10},{3,11},{4,12},{5,13},{6,14},{7,15},{8,0},{9,1},... | collective-permute-start | bytes 393224 | tf_op jit(solution)/shard_map/ppermute | solution.py:52
  60.4 9.1 %collective-permute-start.17 = (f32[256,128]{1,0:T(8,128)S(1)}, f32[256,128]{1,0:T(8,128)S(1)}, u32[]{:S(2)}, u32[]{:S(2)}) collective-permute-start(f32[256,128]{1,0:T(8,128)S(1)} %get-tuple-element.133), channel_id=1, source_target_pairs={{0,4},{1,5},{2,6},{3,7},{4,8},{5,9},{6,10},{7,11},{8,12},{9,13},{1... | collective-permute-start | bytes 393224 | tf_op jit(solution)/shard_map/ppermute | solution.py:52
  61.2 8.4 %collective-permute-start.18 = (f32[256,128]{1,0:T(8,128)S(1)}, f32[256,128]{1,0:T(8,128)S(1)}, u32[]{:S(2)}, u32[]{:S(2)}) collective-permute-start(f32[256,128]{1,0:T(8,128)S(1)} %get-tuple-element.134), channel_id=1, source_target_pairs={{0,12},{1,13},{2,14},{3,15},{4,0},{5,1},{6,2},{7,3},{8,4},{9,5},{1... | collective-permute-start | bytes 393224 | tf_op jit(solution)/shard_map/ppermute | solution.py:52
  69.6 10.4 %collective-permute-start.20 = (f32[256,128]{1,0:T(8,128)S(1)}, f32[256,128]{1,0:T(8,128)S(1)}, u32[]{:S(2)}, u32[]{:S(2)}) collective-permute-start(f32[256,128]{1,0:T(8,128)S(1)} %shard_map.81.refs_12_), channel_id=1, source_target_pairs={{0,242},{1,243},{2,240},{3,241},{4,246},{5,247},{6,244},{7,245},{8... | collective-permute-start | bytes 393224 | tf_op jit(solution)/shard_map/ppermute | solution.py:52
  73.2 8.0 %collective-permute-start.19 = (f32[256,128]{1,0:T(8,128)S(1)}, f32[256,128]{1,0:T(8,128)S(1)}, u32[]{:S(2)}, u32[]{:S(2)}) collective-permute-start(f32[256,128]{1,0:T(8,128)S(1)} %shard_map.81.refs_12_), channel_id=1, source_target_pairs={{0,240},{1,241},{2,242},{3,243},{4,244},{5,245},{6,246},{7,247},{8... | collective-permute-start | bytes 393224 | tf_op jit(solution)/shard_map/ppermute | solution.py:52
  81.2 5.0 %collective-permute-start.23 = (f32[256,128]{1,0:T(8,128)S(1)}, f32[256,128]{1,0:T(8,128)S(1)}, u32[]{:S(2)}, u32[]{:S(2)}) collective-permute-start(f32[256,128]{1,0:T(8,128)S(1)} %shard_map.83.refs_0_.own), channel_id=1, source_target_pairs={{0,12},{1,13},{2,14},{3,15},{4,0},{5,1},{6,2},{7,3},{8,4},{9,5},{1... | collective-permute-start | bytes 393224 | tf_op jit(solution)/shard_map/ppermute | solution.py:52
  81.8 6.6 %collective-permute-start.22 = (f32[256,128]{1,0:T(8,128)S(1)}, f32[256,128]{1,0:T(8,128)S(1)}, u32[]{:S(2)}, u32[]{:S(2)}) collective-permute-start(f32[256,128]{1,0:T(8,128)S(1)} %shard_map.83.refs_0_.own), channel_id=1, source_target_pairs={{0,8},{1,9},{2,10},{3,11},{4,12},{5,13},{6,14},{7,15},{8,0},{9,1},... | collective-permute-start | bytes 393224 | tf_op jit(solution)/shard_map/ppermute | solution.py:52
  82.6 7.2 %collective-permute-start.26 = (f32[256,128]{1,0:T(8,128)S(1)}, f32[256,128]{1,0:T(8,128)S(1)}, u32[]{:S(2)}, u32[]{:S(2)}) collective-permute-start(f32[256,128]{1,0:T(8,128)S(1)} %shard_map.83.refs_0_.own), channel_id=1, source_target_pairs={{0,4},{1,5},{2,6},{3,7},{4,8},{5,9},{6,10},{7,11},{8,12},{9,13},{1... | collective-permute-start | bytes 393224 | tf_op jit(solution)/shard_map/ppermute | solution.py:52
  83.8 6.0 %collective-permute-start.21 = (f32[256,128]{1,0:T(8,128)S(1)}, f32[256,128]{1,0:T(8,128)S(1)}, u32[]{:S(2)}, u32[]{:S(2)}) collective-permute-start(f32[256,128]{1,0:T(8,128)S(1)} %shard_map.83.refs_0_.own), channel_id=1, source_target_pairs={{0,1},{1,0},{2,3},{3,2},{4,5},{5,4},{6,7},{7,6},{8,9},{9,8},{10,11... | collective-permute-start | bytes 393224 | tf_op jit(solution)/shard_map/ppermute | solution.py:52
  86.3 5.5 %collective-permute-start.25 = (f32[256,128]{1,0:T(8,128)S(1)}, f32[256,128]{1,0:T(8,128)S(1)}, u32[]{:S(2)}, u32[]{:S(2)}) collective-permute-start(f32[256,128]{1,0:T(8,128)S(1)} %collective-permute-done.23.refs_1_), channel_id=1, source_target_pairs={{0,1},{1,0},{2,3},{3,2},{4,5},{5,4},{6,7},{7,6},{8,9},{9,8},{10,11... | collective-permute-start | bytes 393224 | tf_op jit(solution)/shard_map/ppermute | solution.py:52
  89.8 6.1 %collective-permute-start.27 = (f32[256,128]{1,0:T(8,128)S(1)}, f32[256,128]{1,0:T(8,128)S(1)}, u32[]{:S(2)}, u32[]{:S(2)}) collective-permute-start(f32[256,128]{1,0:T(8,128)S(1)} %collective-permute-done.26.refs_0_), channel_id=1, source_target_pairs={{0,1},{1,0},{2,3},{3,2},{4,5},{5,4},{6,7},{7,6},{8,9},{9,8},{10,11... | collective-permute-start | bytes 393224 | tf_op jit(solution)/shard_map/ppermute | solution.py:52
  98.0 8.0 %collective-permute-start.30 = (f32[256,128]{1,0:T(8,128)S(1)}, f32[256,128]{1,0:T(8,128)S(1)}, u32[]{:S(2)}, u32[]{:S(2)}) collective-permute-start(f32[256,128]{1,0:T(8,128)S(1)} %get-tuple-element.163), channel_id=1, source_target_pairs={{0,8},{1,9},{2,10},{3,11},{4,12},{5,13},{6,14},{7,15},{8,0},{9,1},... | collective-permute-start | bytes 393224 | tf_op jit(solution)/shard_map/ppermute | solution.py:52
  98.9 9.4 %collective-permute-start.31 = (f32[256,128]{1,0:T(8,128)S(1)}, f32[256,128]{1,0:T(8,128)S(1)}, u32[]{:S(2)}, u32[]{:S(2)}) collective-permute-start(f32[256,128]{1,0:T(8,128)S(1)} %get-tuple-element.164), channel_id=1, source_target_pairs={{0,4},{1,5},{2,6},{3,7},{4,8},{5,9},{6,10},{7,11},{8,12},{9,13},{1... | collective-permute-start | bytes 393224 | tf_op jit(solution)/shard_map/ppermute | solution.py:52
  100.5 7.8 %collective-permute-start.32 = (f32[256,128]{1,0:T(8,128)S(1)}, f32[256,128]{1,0:T(8,128)S(1)}, u32[]{:S(2)}, u32[]{:S(2)}) collective-permute-start(f32[256,128]{1,0:T(8,128)S(1)} %get-tuple-element.165), channel_id=1, source_target_pairs={{0,12},{1,13},{2,14},{3,15},{4,0},{5,1},{6,2},{7,3},{8,4},{9,5},{1... | collective-permute-start | bytes 393224 | tf_op jit(solution)/shard_map/ppermute | solution.py:52
  108.3 15.6 %collective-permute-start.34 = (f32[256,128]{1,0:T(8,128)S(1)}, f32[256,128]{1,0:T(8,128)S(1)}, u32[]{:S(2)}, u32[]{:S(2)}) collective-permute-start(f32[256,128]{1,0:T(8,128)S(1)} %shard_map.89.refs_12_), channel_id=1, source_target_pairs={{0,34},{1,35},{2,32},{3,33},{4,38},{5,39},{6,36},{7,37},{8,42},{9,... | collective-permute-start | bytes 393224 | tf_op jit(solution)/shard_map/ppermute | solution.py:52
  114.1 13.0 %collective-permute-start.33 = (f32[256,128]{1,0:T(8,128)S(1)}, f32[256,128]{1,0:T(8,128)S(1)}, u32[]{:S(2)}, u32[]{:S(2)}) collective-permute-start(f32[256,128]{1,0:T(8,128)S(1)} %shard_map.89.refs_12_), channel_id=1, source_target_pairs={{0,32},{1,33},{2,34},{3,35},{4,36},{5,37},{6,38},{7,39},{8,40},{9,... | collective-permute-start | bytes 393224 | tf_op jit(solution)/shard_map/ppermute | solution.py:52
  127.2 9.5 %collective-permute-start.37 = (f32[128,256]{1,0:T(8,128)S(1)}, f32[128,256]{1,0:T(8,128)S(1)}, u32[]{:S(2)}, u32[]{:S(2)}) collective-permute-start(f32[128,256]{1,0:T(8,128)S(1)} %shard_map.91.refs_0_), channel_id=1, source_target_pairs={{0,4},{1,5},{2,6},{3,7},{4,8},{5,9},{6,10},{7,11},{8,12},{9,13},{1... | collective-permute-start | bytes 393224 | tf_op jit(solution)/shard_map/ppermute | solution.py:52
  127.3 9.4 %collective-permute-start.36 = (f32[128,256]{1,0:T(8,128)S(1)}, f32[128,256]{1,0:T(8,128)S(1)}, u32[]{:S(2)}, u32[]{:S(2)}) collective-permute-start(f32[128,256]{1,0:T(8,128)S(1)} %shard_map.91.refs_0_), channel_id=1, source_target_pairs={{0,8},{1,9},{2,10},{3,11},{4,12},{5,13},{6,14},{7,15},{8,0},{9,1},... | collective-permute-start | bytes 393224 | tf_op jit(solution)/shard_map/ppermute | solution.py:52
  129.7 7.6 %collective-permute-start.35 = (f32[128,256]{1,0:T(8,128)S(1)}, f32[128,256]{1,0:T(8,128)S(1)}, u32[]{:S(2)}, u32[]{:S(2)}) collective-permute-start(f32[128,256]{1,0:T(8,128)S(1)} %shard_map.91.refs_0_), channel_id=1, source_target_pairs={{0,12},{1,13},{2,14},{3,15},{4,0},{5,1},{6,2},{7,3},{8,4},{9,5},{1... | collective-permute-start | bytes 393224 | tf_op jit(solution)/shard_map/ppermute | solution.py:52
  (14 other events, 156.9 us)
where the time goes:
time: 142 us; the launch traced here: 141 us
  waiting for transfers between devices  52.4 us (37%)
  starting transfers between devices  50.6 us (36%)
  Pallas kernels  30.4 us (21%)
  local copies, waits for them, and re-layouts  6.09 us (4%)
    ppermute x39, waiting for transfers between devices, moved(): return lax.ppermute(value, BOTH, pairs)  52.4 us
    ppermute x39, starting transfers between devices, moved(): return lax.ppermute(value, BOTH, pairs)  50.6 us
    pallas_call x26, Pallas kernels, call(): pl.pallas_call(kernel, out_shape=out, in_specs=in_specs, out_specs=out_sp...  30.4 us
    unnamed x15, local copies, waits for them, and re-layouts  3.12 us
  transfers between devices with their start and end apart: 39, of which 21 were waited for; matrix products, arithmetic and copies ran while one was open for 0% of the time, Pallas kernels for 18%

commit v1 on v0

--- a/solution.py
+++ b/solution.py
@@ -23,7 +23,7 @@
 ROW_TILE = 256
 BOTH = ("blk", "rep")
 ORDER = (2, 1, 3)
-CALLS = (((2, 1), (3, 0)), ((0,), (2, 1), (3,)), ((0,), (2, 1), (3,)))
+CALLS = (((2,), (0,), (1, 3)), ((0,), (2,), (1, 3)), ((0,), (2,), (1, 3)))
 
 
 VMEM = pl.BlockSpec(memory_space=pltpu.VMEM)
@@ -84,7 +84,7 @@
     )(*args)
 
 
-def prepare_kernel(pixels, scene, uh, ul, uth, utl, vh, vl, own):
+def prepare_kernel(pixels, scene, before, uh, ul, uth, utl, vh, vl, own):
     core, y = position()
     for r in range(N_Y):
         at = lax.rem(y + r, N_Y) * PAIR
@@ -97,10 +97,10 @@
         uth[:, rows], utl[:, rows] = split(value.T)
 
 
-def prepare(pixels, scene):
+def prepare(pixels, scene, before):
     blocks = jax.ShapeDtypeStruct((N_Y, R, PAIR), BF16)
     out = [HALF, HALF, TURNED, TURNED, blocks, blocks, PIECE]
-    res = call(prepare_kernel, out, [VMEM] * 2, [VMEM] * len(out), (pixels, scene))
+    res = call(prepare_kernel, out, [VMEM] * 2 + [ANY], [VMEM] * len(out), (pixels, scene, before))
     return res[:4], res[4:6], res[6]
 
 
@@ -206,14 +206,14 @@
     return res[0], res[1], res[2:]
 
 
-def add_kernel(*refs):
-    kept, swapped, first, second = refs[:-3], *refs[-3:]
-    first[...] = kept[0][0] + swapped[0]
-    second[...] = kept[-1][-1 % kept[-1].shape[0]] + swapped[1]
-
-
-def add_pair(kept, swapped):
-    return call(add_kernel, [PIECE] * 2, [VMEM] * (len(kept) + 1), [VMEM] * 2, (*kept, swapped))
+def add_first_kernel(kept, swapped, out):
+    out[...] = kept[0] + swapped[0]
+
+
+def add_rest_kernel(kept, own, swapped, first, second, third):
+    first[...] = kept[0] + swapped[0]
+    second[...] = kept[1] + swapped[1]
+    third[...] = own[0] + swapped[2]
 
 
 def total_kernel(own, summed, first, second, third, out):
@@ -247,27 +247,36 @@
 
 def steps(pixel_factors, scene_factors, elevations, quality, occupancy):
     pixels = pixel_factors
-    factors, blocks, own = prepare(pixel_factors, scene_factors)
     tiles = elevations[0], quality[0]
+    factors, blocks, own = prepare(pixel_factors, scene_factors, tiles[0])
     mine = other = None
     for step in range(STEPS):
         last = step + 1 == STEPS
-        parts = []
+        parts, whole = [], CALLS[step].index((0,))
         for n, chunks in enumerate(CALLS[step]):
             block = [mine[r] for r in chunks] + [other[r] for r in chunks] if step else blocks
-            carried = [parts[0][0]] if step and n == 2 else []
             before = [parts[-1][1]] if parts else []
+            if n == 2:
+                carried, before = [parts[whole][0]], [*before, sums]
+            else:
+                carried = []
             parts.append(misfit_part(step, chunks, occupancy, factors, tiles, block, carried, before))
+            if chunks == (2,):
+                early = moved(parts[-1][0], core=1)
+                sums = call(add_first_kernel, PIECE, [VMEM] * 2, VMEM, (parts[-1][1], early))
+                arrived = [moved(sums, y=2)]
         if step:
             blocks = [p[4] for p in parts] + [p[5] for p in parts]
-        kept = [p[1] for p in parts]
-        early = moved(parts[-2][0], core=1)
-        late = moved(parts[-1][0], core=1)
-        sums = add_pair(kept[-2:-1], early)
-        arrived = [moved(v, y=r) for r, v in zip(ORDER, sums)]
-        sums = add_pair([kept[-1], kept[0]] if step else kept[-1:], late)
-        arrived.append(moved(sums[0], y=ORDER[2]))
-        half = call(total_kernel, PIECE, [VMEM] * 5, VMEM, (own, sums[1], *arrived))
+        late = moved(parts[2][0], core=1)
+        sums = call(
+            add_rest_kernel,
+            [PIECE] * 3,
+            [VMEM] * 3,
+            [VMEM] * 3,
+            (parts[2][1], parts[whole][1], late),
+        )
+        arrived += [moved(v, y=r) for r, v in zip((1, 3), sums)]
+        half = call(total_kernel, PIECE, [VMEM] * 5, VMEM, (own, sums[2], *arrived))
         go = STEPS - 1 if last else -1
         far, near = moved(half, blk=go, zh=1), moved(half, blk=go)
         token, pixels, factors = pixel_step(step, pixels, parts, blocks, half)

time: 142 us -> 137 us (0.965)
  waiting for transfers between devices: 52.4 us -> 37.8 us
  starting transfers between devices: 50.6 us -> 62.4 us
  local copies, waits for them, and re-layouts: 6.09 us -> 3.64 us
    ppermute x39, waiting for transfers between devices: 52.4 us -> 37.8 us  [moved(): return lax.ppermute(value, BOTH, pairs)]
    ppermute x39, starting transfers between devices: 50.6 us -> 62.4 us  [moved(): return lax.ppermute(value, BOTH, pairs)]
    unnamed x15 -> x13, local copies, waits for them, and re-layouts: 3.12 us -> 0.84 us
    pallas_call x26 -> x27, Pallas kernels: 30.4 us -> 31 us  [call(): pl.pallas_call(kernel, out_shape=out, in_specs=in_specs, out_specs=out_sp...]
  transfers between devices with their start and end apart: 39 -> 39, of which waited for: 21 -> 27; matrix products, arithmetic and copies ran while one was open for 0% -> 0% of each run, Pallas kernels for 18% -> 12%
where the time goes in v1:
time: 137 us; the launch traced here: 136 us
  starting transfers between devices  62.4 us (46%)
  waiting for transfers between devices  37.8 us (28%)
  Pallas kernels  31 us (23%)
  local copies, waits for them, and re-layouts  3.64 us (3%)
    ppermute x39, starting transfers between devices, moved(): return lax.ppermute(value, BOTH, pairs)  62.4 us
    ppermute x39, waiting for transfers between devices, moved(): return lax.ppermute(value, BOTH, pairs)  37.8 us
    pallas_call x27, Pallas kernels, call(): pl.pallas_call(kernel, out_shape=out, in_specs=in_specs, out_specs=out_sp...  31 us
  transfers between devices with their start and end apart: 39, of which 27 were waited for; matrix products, arithmetic and copies ran while one was open for 0% of the time, Pallas kernels for 12%

profile of v1, /device:TPU:2, one launch (start us, length us, event | category | flops | bytes accessed | tf_op | source)
XLA Modules:
  0.0 136.0 jit_solution(4778729249821569570)
XLA Ops:
  1.4 2.3 %slice_bitcast_fusion.4 = (bf16[768,1024]{1,0:T(8,128)(2,1)S(1)}, bf16[768,1024]{1,0:T(8,128)(2,1)S(1)}) fusion(bf16[3,768,1024]{2,1,0:T(8,128)(2,1)} %param.8, bf16[3,768,1024]{2,1,0:T(8,128)(2,1)} %param.7), kind=kLoop, calls=%fused_computation.4 | loop fusion | bytes 6291456 | tf_op jit(solution)/shard_map/squeeze | solution.py:250
  8.5 3.4 %shard_map.72 = (f32[3,256,128]{2,1,0:T(8,128)S(1)}, f32[2,256,128]{2,1,0:T(8,128)S(1)}, bf16[2,768,256]{2,1,0:T(8,128)(2,1)S(1)}, bf16[2,768,256]{2,1,0:T(8,128)(2,1)S(1)}) custom-call(s32[3,1]{1,0:T(4,128)S(1)} %copy.7.occupancy, bf16[768,256]{1,0:T(8,128)(2,1)S(1)} %get-tuple-element.86.uh, bf16[768,256]{1,0:T(8,128)(2,1)S(1)} %get-tuple-element.87.ul, ...), custom_call_target="tpu_custom_call" | custom-call | flops 1207959552 | bytes 1048576 | tf_op jit(solution)/shard_map/pallas_call | solution.py:76
  12.4 3.2 %collective-permute-start.2 = (f32[256,128]{1,0:T(8,128)S(1)}, f32[256,128]{1,0:T(8,128)S(1)}, u32[]{:S(2)}, u32[]{:S(2)}) collective-permute-start(f32[256,128]{1,0:T(8,128)S(1)} %shard_map.71.refs_4_), channel_id=1, source_target_pairs={{0,8},{1,9},{2,10},{3,11},{4,12},{5,13},{6,14},{7,15},{8,0},{9,1},... | collective-permute-start | bytes 393224 | tf_op jit(solution)/shard_map/ppermute | solution.py:52
  16.4 2.6 %collective-permute-start.4 = (f32[256,128]{1,0:T(8,128)S(1)}, f32[256,128]{1,0:T(8,128)S(1)}, u32[]{:S(2)}, u32[]{:S(2)}) collective-permute-start(f32[256,128]{1,0:T(8,128)S(1)} %get-tuple-element.107), channel_id=1, source_target_pairs={{0,12},{1,13},{2,14},{3,15},{4,0},{5,1},{6,2},{7,3},{8,4},{9,5},{1... | collective-permute-start | bytes 393224 | tf_op jit(solution)/shard_map/ppermute | solution.py:52
  19.5 2.7 %collective-permute-done.3.second = f32[256,128]{1,0:T(8,128)S(1)} collective-permute-done((f32[256,128]{1,0:T(8,128)S(1)}, f32[256,128]{1,0:T(8,128)S(1)}, u32[]{:S(2)}, u32[]{:S(2)}) %collective-permute-start.3) | collective-permute-done | bytes 131104 | tf_op jit(solution)/shard_map/ppermute | solution.py:52
  22.6 7.2 %collective-permute-start.6 = (f32[256,128]{1,0:T(8,128)S(1)}, f32[256,128]{1,0:T(8,128)S(1)}, u32[]{:S(2)}, u32[]{:S(2)}) collective-permute-start(f32[256,128]{1,0:T(8,128)S(1)} %shard_map.74.refs_8_), channel_id=1, source_target_pairs={{0,242},{1,243},{2,240},{3,241},{4,246},{5,247},{6,244},{7,245},{8... | collective-permute-start | bytes 393224 | tf_op jit(solution)/shard_map/ppermute | solution.py:52
  31.3 2.0 %shard_map.75 = (f32[8,128]{1,0:T(8,128)S(1)}, f32[768,256]{1,0:T(8,128)S(1)}, bf16[768,256]{1,0:T(8,128)(2,1)S(1)}, bf16[768,256]{1,0:T(8,128)(2,1)S(1)}, bf16[...) custom-call(f32[768,256]{1,0:T(8,128)S(1)} %copy-done, bf16[1,768,256]{2,1,0:T(8,128)(2,1)S(1)} %get-tuple-element.92.refs_0_, ...), custom_call_target="tpu_custom_call" | custom-call | flops 1207959552 | bytes 1048576 | tf_op jit(solution)/shard_map/pallas_call | solution.py:76
  33.9 2.7 %collective-permute-done.5.a = f32[256,128]{1,0:T(8,128)S(1)} collective-permute-done((f32[256,128]{1,0:T(8,128)S(1)}, f32[256,128]{1,0:T(8,128)S(1)}, u32[]{:S(2)}, u32[]{:S(2)}) %collective-permute-start.5) | collective-permute-done | bytes 131104 | tf_op jit(solution)/shard_map/ppermute | solution.py:52
  36.7 3.8 %collective-permute-start.8 = (f32[256,128]{1,0:T(8,128)S(1)}, f32[256,128]{1,0:T(8,128)S(1)}, u32[]{:S(2)}, u32[]{:S(2)}) collective-permute-start(f32[256,128]{1,0:T(8,128)S(1)} %shard_map.76.refs_0_.own), channel_id=1, source_target_pairs={{0,8},{1,9},{2,10},{3,11},{4,12},{5,13},{6,14},{7,15},{8,0},{9,1},... | collective-permute-start | bytes 393224 | tf_op jit(solution)/shard_map/ppermute | solution.py:52
  40.8 3.1 %collective-permute-start.10 = (f32[256,128]{1,0:T(8,128)S(1)}, f32[256,128]{1,0:T(8,128)S(1)}, u32[]{:S(2)}, u32[]{:S(2)}) collective-permute-start(f32[256,128]{1,0:T(8,128)S(1)} %shard_map.76.refs_0_.own), channel_id=1, source_target_pairs={{0,12},{1,13},{2,14},{3,15},{4,0},{5,1},{6,2},{7,3},{8,4},{9,5},{1... | collective-permute-start | bytes 393224 | tf_op jit(solution)/shard_map/ppermute | solution.py:52
  51.1 3.5 %shard_map.80 = (f32[3,256,128]{2,1,0:T(8,128)S(1)}, f32[2,256,128]{2,1,0:T(8,128)S(1)}, bf16[2,768,256]{2,1,0:T(8,128)(2,1)S(1)}, bf16[2,768,256]{2,1,0:T(8,128...) custom-call(s32[3,1]{1,0:T(4,128)S(1)} %copy.7.occupancy, ...), custom_call_target="tpu_custom_call" | custom-call | flops 1207959552 | bytes 1048576 | tf_op jit(solution)/shard_map/pallas_call | solution.py:76
  54.9 3.6 %collective-permute-start.16 = (f32[256,128]{1,0:T(8,128)S(1)}, f32[256,128]{1,0:T(8,128)S(1)}, u32[]{:S(2)}, u32[]{:S(2)}) collective-permute-start(f32[256,128]{1,0:T(8,128)S(1)} %shard_map.79.refs_6_), channel_id=1, source_target_pairs={{0,8},{1,9},{2,10},{3,11},{4,12},{5,13},{6,14},{7,15},{8,0},{9,1},... | collective-permute-start | bytes 393224 | tf_op jit(solution)/shard_map/ppermute | solution.py:52
  58.7 3.1 %collective-permute-start.18 = (f32[256,128]{1,0:T(8,128)S(1)}, f32[256,128]{1,0:T(8,128)S(1)}, u32[]{:S(2)}, u32[]{:S(2)}) collective-permute-start(f32[256,128]{1,0:T(8,128)S(1)} %get-tuple-element.137), channel_id=1, source_target_pairs={{0,12},{1,13},{2,14},{3,15},{4,0},{5,1},{6,2},{7,3},{8,4},{9,5},{1... | collective-permute-start | bytes 393224 | tf_op jit(solution)/shard_map/ppermute | solution.py:52
  62.9 2.6 %collective-permute-done.17.second = f32[256,128]{1,0:T(8,128)S(1)} collective-permute-done((f32[256,128]{1,0:T(8,128)S(1)}, f32[256,128]{1,0:T(8,128)S(1)}, u32[]{:S(2)}, u32[]{:S(2)}) %collective-permute-start.17) | collective-permute-done | bytes 131104 | tf_op jit(solution)/shard_map/ppermute | solution.py:52
  65.5 4.4 %collective-permute-start.20 = (f32[256,128]{1,0:T(8,128)S(1)}, f32[256,128]{1,0:T(8,128)S(1)}, u32[]{:S(2)}, u32[]{:S(2)}) collective-permute-start(f32[256,128]{1,0:T(8,128)S(1)} %shard_map.82.refs_12_), channel_id=1, source_target_pairs={{0,242},{1,243},{2,240},{3,241},{4,246},{5,247},{6,244},{7,245},{8... | collective-permute-start | bytes 393224 | tf_op jit(solution)/shard_map/ppermute | solution.py:52
  71.2 2.0 %shard_map.83 = (f32[8,128]{1,0:T(8,128)S(1)}, f32[768,256]{1,0:T(8,128)S(1)}, bf16[768,256]{1,0:T(8,128)(2,1)S(1)}, bf16[768,256]{1,0:T(8,128)(2,1)S(1)}, bf16[...) custom-call(f32[768,256]{1,0:T(8,128)S(1)} %get-tuple-element.108.pixels, ...), custom_call_target="tpu_custom_call" | custom-call | flops 1207959552 | bytes 1048576 | tf_op jit(solution)/shard_map/pallas_call | solution.py:76
  73.3 2.1 %collective-permute-done.20.b = f32[256,128]{1,0:T(8,128)S(1)} collective-permute-done((f32[256,128]{1,0:T(8,128)S(1)}, f32[256,128]{1,0:T(8,128)S(1)}, u32[]{:S(2)}, u32[]{:S(2)}) %collective-permute-start.20) | collective-permute-done | bytes 131104 | tf_op jit(solution)/shard_map/ppermute | solution.py:52
  75.4 2.2 %collective-permute-done.19.a = f32[256,128]{1,0:T(8,128)S(1)} collective-permute-done((f32[256,128]{1,0:T(8,128)S(1)}, f32[256,128]{1,0:T(8,128)S(1)}, u32[]{:S(2)}, u32[]{:S(2)}) %collective-permute-start.19) | collective-permute-done | bytes 131104 | tf_op jit(solution)/shard_map/ppermute | solution.py:52
  77.6 2.4 %collective-permute-start.22 = (f32[256,128]{1,0:T(8,128)S(1)}, f32[256,128]{1,0:T(8,128)S(1)}, u32[]{:S(2)}, u32[]{:S(2)}) collective-permute-start(f32[256,128]{1,0:T(8,128)S(1)} %shard_map.84.refs_0_.own), channel_id=1, source_target_pairs={{0,8},{1,9},{2,10},{3,11},{4,12},{5,13},{6,14},{7,15},{8,0},{9,1},... | collective-permute-start | bytes 393224 | tf_op jit(solution)/shard_map/ppermute | solution.py:52
  80.3 3.2 %collective-permute-start.24 = (f32[256,128]{1,0:T(8,128)S(1)}, f32[256,128]{1,0:T(8,128)S(1)}, u32[]{:S(2)}, u32[]{:S(2)}) collective-permute-start(f32[256,128]{1,0:T(8,128)S(1)} %shard_map.84.refs_0_.own), channel_id=1, source_target_pairs={{0,12},{1,13},{2,14},{3,15},{4,0},{5,1},{6,2},{7,3},{8,4},{9,5},{1... | collective-permute-start | bytes 393224 | tf_op jit(solution)/shard_map/ppermute | solution.py:52
  83.5 2.1 %collective-permute-done.22.refs_0_ = f32[256,128]{1,0:T(8,128)S(1)} collective-permute-done((f32[256,128]{1,0:T(8,128)S(1)}, f32[256,128]{1,0:T(8,128)S(1)}, u32[]{:S(2)}, u32[]{:S(2)}) %collective-permute-start.22) | collective-permute-done | bytes 131104 | tf_op jit(solution)/shard_map/ppermute | solution.py:52
  91.8 3.4 %shard_map.88 = (f32[3,256,128]{2,1,0:T(8,128)S(1)}, f32[2,256,128]{2,1,0:T(8,128)S(1)}, bf16[2,768,256]{2,1,0:T(8,128)(2,1)S(1)}, bf16[2,768,256]{2,1,0:T(8,128...) custom-call(s32[3,1]{1,0:T(4,128)S(1)} %copy.7.occupancy, ...), custom_call_target="tpu_custom_call" | custom-call | flops 1207959552 | bytes 1048576 | tf_op jit(solution)/shard_map/pallas_call | solution.py:76
  98.1 2.3 %collective-permute-start.32 = (f32[256,128]{1,0:T(8,128)S(1)}, f32[256,128]{1,0:T(8,128)S(1)}, u32[]{:S(2)}, u32[]{:S(2)}) collective-permute-start(f32[256,128]{1,0:T(8,128)S(1)} %get-tuple-element.167), channel_id=1, source_target_pairs={{0,12},{1,13},{2,14},{3,15},{4,0},{5,1},{6,2},{7,3},{8,4},{9,5},{1... | collective-permute-start | bytes 393224 | tf_op jit(solution)/shard_map/ppermute | solution.py:52
  100.4 3.1 %collective-permute-done.30.first = f32[256,128]{1,0:T(8,128)S(1)} collective-permute-done((f32[256,128]{1,0:T(8,128)S(1)}, f32[256,128]{1,0:T(8,128)S(1)}, u32[]{:S(2)}, u32[]{:S(2)}) %collective-permute-start.30) | collective-permute-done | bytes 131104 | tf_op jit(solution)/shard_map/ppermute | solution.py:52
  105.6 5.2 %collective-permute-start.34 = (f32[256,128]{1,0:T(8,128)S(1)}, f32[256,128]{1,0:T(8,128)S(1)}, u32[]{:S(2)}, u32[]{:S(2)}) collective-permute-start(f32[256,128]{1,0:T(8,128)S(1)} %shard_map.90.refs_12_), channel_id=1, source_target_pairs={{0,34},{1,35},{2,32},{3,33},{4,38},{5,39},{6,36},{7,37},{8,42},{9,... | collective-permute-start | bytes 393224 | tf_op jit(solution)/shard_map/ppermute | solution.py:52
  110.8 2.7 %collective-permute-start.33 = (f32[256,128]{1,0:T(8,128)S(1)}, f32[256,128]{1,0:T(8,128)S(1)}, u32[]{:S(2)}, u32[]{:S(2)}) collective-permute-start(f32[256,128]{1,0:T(8,128)S(1)} %shard_map.90.refs_12_), channel_id=1, source_target_pairs={{0,32},{1,33},{2,34},{3,35},{4,36},{5,37},{6,38},{7,39},{8,40},{9,... | collective-permute-start | bytes 393224 | tf_op jit(solution)/shard_map/ppermute | solution.py:52
  113.5 2.7 %shard_map.91 = (f32[8,128]{1,0:T(8,128)S(1)}, f32[768,256]{1,0:T(8,128)}) custom-call(f32[768,256]{1,0:T(8,128)S(1)} %get-tuple-element.138.pixels, bf16[1,768,256]{2,1,0:T(8,128)(2,1)S(1)} %get-tuple-element.147.refs_0_, bf16[1,768,256]{2,1,0:T(8,128)(2,1)S(1)} %get-tuple-element.149.refs_1_, bf16[2,768,256]{2,1,0:T(8,128)(2,1)S(1)} %get-tuple-element.153.refs_2_, ...), custom_call_target="tpu_custom_call" | custom-call | flops 1207959552 | bytes 1048576 | tf_op jit(solution)/shard_map/pallas_call | solution.py:76
  116.2 4.6 %collective-permute-done.34.b = f32[256,128]{1,0:T(8,128)S(1)} collective-permute-done((f32[256,128]{1,0:T(8,128)S(1)}, f32[256,128]{1,0:T(8,128)S(1)}, u32[]{:S(2)}, u32[]{:S(2)}) %collective-permute-start.34) | collective-permute-done | bytes 131104 | tf_op jit(solution)/shard_map/ppermute | solution.py:52
  120.8 2.1 %collective-permute-done.33.a = f32[256,128]{1,0:T(8,128)S(1)} collective-permute-done((f32[256,128]{1,0:T(8,128)S(1)}, f32[256,128]{1,0:T(8,128)S(1)}, u32[]{:S(2)}, u32[]{:S(2)}) %collective-permute-start.33) | collective-permute-done | bytes 131104 | tf_op jit(solution)/shard_map/ppermute | solution.py:52
  124.5 2.2 %collective-permute-start.36 = (f32[128,256]{1,0:T(8,128)S(1)}, f32[128,256]{1,0:T(8,128)S(1)}, u32[]{:S(2)}, u32[]{:S(2)}) collective-permute-start(f32[128,256]{1,0:T(8,128)S(1)} %shard_map.92.refs_0_), channel_id=1, source_target_pairs={{0,8},{1,9},{2,10},{3,11},{4,12},{5,13},{6,14},{7,15},{8,0},{9,1},... | collective-permute-start | bytes 393224 | tf_op jit(solution)/shard_map/ppermute | solution.py:52
  126.7 2.5 %collective-permute-start.35 = (f32[128,256]{1,0:T(8,128)S(1)}, f32[128,256]{1,0:T(8,128)S(1)}, u32[]{:S(2)}, u32[]{:S(2)}) collective-permute-start(f32[128,256]{1,0:T(8,128)S(1)} %shard_map.92.refs_0_), channel_id=1, source_target_pairs={{0,12},{1,13},{2,14},{3,15},{4,0},{5,1},{6,2},{7,3},{8,4},{9,5},{1... | collective-permute-start | bytes 393224 | tf_op jit(solution)/shard_map/ppermute | solution.py:52
  130.1 2.5 %collective-permute-done.36.refs_2_ = f32[128,256]{1,0:T(8,128)S(1)} collective-permute-done((f32[128,256]{1,0:T(8,128)S(1)}, f32[128,256]{1,0:T(8,128)S(1)}, u32[]{:S(2)}, u32[]{:S(2)}) %collective-permute-start.36) | collective-permute-done | bytes 131104 | tf_op jit(solution)/shard_map/ppermute | solution.py:52
  (93 shorter events, 37.2 us)
Async XLA Ops:
  6.3 2.1 %collective-permute-start = (f32[1,256,128]{2,1,0:T(8,128)S(1)}, f32[1,256,128]{2,1,0:T(8,128)S(1)}, u32[]{:S(2)}, u32[]{:S(2)}) collective-permute-start(f32[1,256,128]{2,1,0:T(8,128)S(1)} %get-tuple-element.97), channel_id=1, source_target_pairs={{0,1},{1,0},{2,3},{3,2},{4,5},{5,4},{6,7},{7,6},{8,9},{9,8},{10,11... | collective-permute-start | bytes 393224 | tf_op jit(solution)/shard_map/ppermute | solution.py:52
  11.9 3.8 %collective-permute-start.1 = (f32[3,256,128]{2,1,0:T(8,128)S(1)}, f32[3,256,128]{2,1,0:T(8,128)S(1)}, u32[]{:S(2)}, u32[]{:S(2)}) collective-permute-start(f32[3,256,128]{2,1,0:T(8,128)S(1)} %get-tuple-element.104), channel_id=1, source_target_pairs={{0,1},{1,0},{2,3},{3,2},{4,5},{5,4},{6,7},{7,6},{8,9},{9,8},{10,11... | collective-permute-start | bytes 1179656 | tf_op jit(solution)/shard_map/ppermute | solution.py:52
  12.4 7.1 %collective-permute-start.2 = (f32[256,128]{1,0:T(8,128)S(1)}, f32[256,128]{1,0:T(8,128)S(1)}, u32[]{:S(2)}, u32[]{:S(2)}) collective-permute-start(f32[256,128]{1,0:T(8,128)S(1)} %shard_map.71.refs_4_), channel_id=1, source_target_pairs={{0,8},{1,9},{2,10},{3,11},{4,12},{5,13},{6,14},{7,15},{8,0},{9,1},... | collective-permute-start | bytes 393224 | tf_op jit(solution)/shard_map/ppermute | solution.py:52
  15.7 6.6 %collective-permute-start.3 = (f32[256,128]{1,0:T(8,128)S(1)}, f32[256,128]{1,0:T(8,128)S(1)}, u32[]{:S(2)}, u32[]{:S(2)}) collective-permute-start(f32[256,128]{1,0:T(8,128)S(1)} %get-tuple-element.106), channel_id=1, source_target_pairs={{0,4},{1,5},{2,6},{3,7},{4,8},{5,9},{6,10},{7,11},{8,12},{9,13},{1... | collective-permute-start | bytes 393224 | tf_op jit(solution)/shard_map/ppermute | solution.py:52
  16.4 6.2 %collective-permute-start.4 = (f32[256,128]{1,0:T(8,128)S(1)}, f32[256,128]{1,0:T(8,128)S(1)}, u32[]{:S(2)}, u32[]{:S(2)}) collective-permute-start(f32[256,128]{1,0:T(8,128)S(1)} %get-tuple-element.107), channel_id=1, source_target_pairs={{0,12},{1,13},{2,14},{3,15},{4,0},{5,1},{6,2},{7,3},{8,4},{9,5},{1... | collective-permute-start | bytes 393224 | tf_op jit(solution)/shard_map/ppermute | solution.py:52
  22.6 11.3 %collective-permute-start.6 = (f32[256,128]{1,0:T(8,128)S(1)}, f32[256,128]{1,0:T(8,128)S(1)}, u32[]{:S(2)}, u32[]{:S(2)}) collective-permute-start(f32[256,128]{1,0:T(8,128)S(1)} %shard_map.74.refs_8_), channel_id=1, source_target_pairs={{0,242},{1,243},{2,240},{3,241},{4,246},{5,247},{6,244},{7,245},{8... | collective-permute-start | bytes 393224 | tf_op jit(solution)/shard_map/ppermute | solution.py:52
  29.9 6.8 %collective-permute-start.5 = (f32[256,128]{1,0:T(8,128)S(1)}, f32[256,128]{1,0:T(8,128)S(1)}, u32[]{:S(2)}, u32[]{:S(2)}) collective-permute-start(f32[256,128]{1,0:T(8,128)S(1)} %shard_map.74.refs_8_), channel_id=1, source_target_pairs={{0,240},{1,241},{2,242},{3,243},{4,244},{5,245},{6,246},{7,247},{8... | collective-permute-start | bytes 393224 | tf_op jit(solution)/shard_map/ppermute | solution.py:52
  36.7 8.1 %collective-permute-start.8 = (f32[256,128]{1,0:T(8,128)S(1)}, f32[256,128]{1,0:T(8,128)S(1)}, u32[]{:S(2)}, u32[]{:S(2)}) collective-permute-start(f32[256,128]{1,0:T(8,128)S(1)} %shard_map.76.refs_0_.own), channel_id=1, source_target_pairs={{0,8},{1,9},{2,10},{3,11},{4,12},{5,13},{6,14},{7,15},{8,0},{9,1},... | collective-permute-start | bytes 393224 | tf_op jit(solution)/shard_map/ppermute | solution.py:52
  40.5 9.0 %collective-permute-start.11 = (f32[256,128]{1,0:T(8,128)S(1)}, f32[256,128]{1,0:T(8,128)S(1)}, u32[]{:S(2)}, u32[]{:S(2)}) collective-permute-start(f32[256,128]{1,0:T(8,128)S(1)} %shard_map.76.refs_0_.own), channel_id=1, source_target_pairs={{0,4},{1,5},{2,6},{3,7},{4,8},{5,9},{6,10},{7,11},{8,12},{9,13},{1... | collective-permute-start | bytes 393224 | tf_op jit(solution)/shard_map/ppermute | solution.py:52
  40.8 9.0 %collective-permute-start.10 = (f32[256,128]{1,0:T(8,128)S(1)}, f32[256,128]{1,0:T(8,128)S(1)}, u32[]{:S(2)}, u32[]{:S(2)}) collective-permute-start(f32[256,128]{1,0:T(8,128)S(1)} %shard_map.76.refs_0_.own), channel_id=1, source_target_pairs={{0,12},{1,13},{2,14},{3,15},{4,0},{5,1},{6,2},{7,3},{8,4},{9,5},{1... | collective-permute-start | bytes 393224 | tf_op jit(solution)/shard_map/ppermute | solution.py:52
  44.8 2.4 %collective-permute-start.9 = (f32[256,128]{1,0:T(8,128)S(1)}, f32[256,128]{1,0:T(8,128)S(1)}, u32[]{:S(2)}, u32[]{:S(2)}) collective-permute-start(f32[256,128]{1,0:T(8,128)S(1)} %collective-permute-done.8.refs_0_), channel_id=1, source_target_pairs={{0,1},{1,0},{2,3},{3,2},{4,5},{5,4},{6,7},{7,6},{8,9},{9,8},{10,11... | collective-permute-start | bytes 393224 | tf_op jit(solution)/shard_map/ppermute | solution.py:52
  54.6 3.9 %collective-permute-start.15 = (f32[3,256,128]{2,1,0:T(8,128)S(1)}, f32[3,256,128]{2,1,0:T(8,128)S(1)}, u32[]{:S(2)}, u32[]{:S(2)}) collective-permute-start(f32[3,256,128]{2,1,0:T(8,128)S(1)} %get-tuple-element.134), channel_id=1, source_target_pairs={{0,1},{1,0},{2,3},{3,2},{4,5},{5,4},{6,7},{7,6},{8,9},{9,8},{10,11... | collective-permute-start | bytes 1179656 | tf_op jit(solution)/shard_map/ppermute | solution.py:52
  54.9 7.9 %collective-permute-start.16 = (f32[256,128]{1,0:T(8,128)S(1)}, f32[256,128]{1,0:T(8,128)S(1)}, u32[]{:S(2)}, u32[]{:S(2)}) collective-permute-start(f32[256,128]{1,0:T(8,128)S(1)} %shard_map.79.refs_6_), channel_id=1, source_target_pairs={{0,8},{1,9},{2,10},{3,11},{4,12},{5,13},{6,14},{7,15},{8,0},{9,1},... | collective-permute-start | bytes 393224 | tf_op jit(solution)/shard_map/ppermute | solution.py:52
  58.6 6.8 %collective-permute-start.17 = (f32[256,128]{1,0:T(8,128)S(1)}, f32[256,128]{1,0:T(8,128)S(1)}, u32[]{:S(2)}, u32[]{:S(2)}) collective-permute-start(f32[256,128]{1,0:T(8,128)S(1)} %get-tuple-element.136), channel_id=1, source_target_pairs={{0,4},{1,5},{2,6},{3,7},{4,8},{5,9},{6,10},{7,11},{8,12},{9,13},{1... | collective-permute-start | bytes 393224 | tf_op jit(solution)/shard_map/ppermute | solution.py:52
  58.7 6.7 %collective-permute-start.18 = (f32[256,128]{1,0:T(8,128)S(1)}, f32[256,128]{1,0:T(8,128)S(1)}, u32[]{:S(2)}, u32[]{:S(2)}) collective-permute-start(f32[256,128]{1,0:T(8,128)S(1)} %get-tuple-element.137), channel_id=1, source_target_pairs={{0,12},{1,13},{2,14},{3,15},{4,0},{5,1},{6,2},{7,3},{8,4},{9,5},{1... | collective-permute-start | bytes 393224 | tf_op jit(solution)/shard_map/ppermute | solution.py:52
  65.5 9.9 %collective-permute-start.20 = (f32[256,128]{1,0:T(8,128)S(1)}, f32[256,128]{1,0:T(8,128)S(1)}, u32[]{:S(2)}, u32[]{:S(2)}) collective-permute-start(f32[256,128]{1,0:T(8,128)S(1)} %shard_map.82.refs_12_), channel_id=1, source_target_pairs={{0,242},{1,243},{2,240},{3,241},{4,246},{5,247},{6,244},{7,245},{8... | collective-permute-start | bytes 393224 | tf_op jit(solution)/shard_map/ppermute | solution.py:52
  69.9 7.8 %collective-permute-start.19 = (f32[256,128]{1,0:T(8,128)S(1)}, f32[256,128]{1,0:T(8,128)S(1)}, u32[]{:S(2)}, u32[]{:S(2)}) collective-permute-start(f32[256,128]{1,0:T(8,128)S(1)} %shard_map.82.refs_12_), channel_id=1, source_target_pairs={{0,240},{1,241},{2,242},{3,243},{4,244},{5,245},{6,246},{7,247},{8... | collective-permute-start | bytes 393224 | tf_op jit(solution)/shard_map/ppermute | solution.py:52
  77.6 8.0 %collective-permute-start.22 = (f32[256,128]{1,0:T(8,128)S(1)}, f32[256,128]{1,0:T(8,128)S(1)}, u32[]{:S(2)}, u32[]{:S(2)}) collective-permute-start(f32[256,128]{1,0:T(8,128)S(1)} %shard_map.84.refs_0_.own), channel_id=1, source_target_pairs={{0,8},{1,9},{2,10},{3,11},{4,12},{5,13},{6,14},{7,15},{8,0},{9,1},... | collective-permute-start | bytes 393224 | tf_op jit(solution)/shard_map/ppermute | solution.py:52
  80.2 10.1 %collective-permute-start.25 = (f32[256,128]{1,0:T(8,128)S(1)}, f32[256,128]{1,0:T(8,128)S(1)}, u32[]{:S(2)}, u32[]{:S(2)}) collective-permute-start(f32[256,128]{1,0:T(8,128)S(1)} %shard_map.84.refs_0_.own), channel_id=1, source_target_pairs={{0,4},{1,5},{2,6},{3,7},{4,8},{5,9},{6,10},{7,11},{8,12},{9,13},{1... | collective-permute-start | bytes 393224 | tf_op jit(solution)/shard_map/ppermute | solution.py:52
  80.3 10.1 %collective-permute-start.24 = (f32[256,128]{1,0:T(8,128)S(1)}, f32[256,128]{1,0:T(8,128)S(1)}, u32[]{:S(2)}, u32[]{:S(2)}) collective-permute-start(f32[256,128]{1,0:T(8,128)S(1)} %shard_map.84.refs_0_.own), channel_id=1, source_target_pairs={{0,12},{1,13},{2,14},{3,15},{4,0},{5,1},{6,2},{7,3},{8,4},{9,5},{1... | collective-permute-start | bytes 393224 | tf_op jit(solution)/shard_map/ppermute | solution.py:52
  83.5 2.2 %collective-permute-start.21 = (f32[256,128]{1,0:T(8,128)S(1)}, f32[256,128]{1,0:T(8,128)S(1)}, u32[]{:S(2)}, u32[]{:S(2)}) collective-permute-start(f32[256,128]{1,0:T(8,128)S(1)} %shard_map.84.refs_0_.own), channel_id=1, source_target_pairs={{0,1},{1,0},{2,3},{3,2},{4,5},{5,4},{6,7},{7,6},{8,9},{9,8},{10,11... | collective-permute-start | bytes 393224 | tf_op jit(solution)/shard_map/ppermute | solution.py:52
  85.6 2.1 %collective-permute-start.23 = (f32[256,128]{1,0:T(8,128)S(1)}, f32[256,128]{1,0:T(8,128)S(1)}, u32[]{:S(2)}, u32[]{:S(2)}) collective-permute-start(f32[256,128]{1,0:T(8,128)S(1)} %collective-permute-done.22.refs_0_), channel_id=1, source_target_pairs={{0,1},{1,0},{2,3},{3,2},{4,5},{5,4},{6,7},{7,6},{8,9},{9,8},{10,11... | collective-permute-start | bytes 393224 | tf_op jit(solution)/shard_map/ppermute | solution.py:52
  95.3 1.8 %collective-permute-start.29 = (f32[3,256,128]{2,1,0:T(8,128)S(1)}, f32[3,256,128]{2,1,0:T(8,128)S(1)}, u32[]{:S(2)}, u32[]{:S(2)}) collective-permute-start(f32[3,256,128]{2,1,0:T(8,128)S(1)} %get-tuple-element.164), channel_id=1, source_target_pairs={{0,1},{1,0},{2,3},{3,2},{4,5},{5,4},{6,7},{7,6},{8,9},{9,8},{10,11... | collective-permute-start | bytes 1179656 | tf_op jit(solution)/shard_map/ppermute | solution.py:52
  95.7 7.9 %collective-permute-start.30 = (f32[256,128]{1,0:T(8,128)S(1)}, f32[256,128]{1,0:T(8,128)S(1)}, u32[]{:S(2)}, u32[]{:S(2)}) collective-permute-start(f32[256,128]{1,0:T(8,128)S(1)} %shard_map.87.refs_6_), channel_id=1, source_target_pairs={{0,8},{1,9},{2,10},{3,11},{4,12},{5,13},{6,14},{7,15},{8,0},{9,1},... | collective-permute-start | bytes 393224 | tf_op jit(solution)/shard_map/ppermute | solution.py:52
  97.1 8.4 %collective-permute-start.31 = (f32[256,128]{1,0:T(8,128)S(1)}, f32[256,128]{1,0:T(8,128)S(1)}, u32[]{:S(2)}, u32[]{:S(2)}) collective-permute-start(f32[256,128]{1,0:T(8,128)S(1)} %get-tuple-element.166), channel_id=1, source_target_pairs={{0,4},{1,5},{2,6},{3,7},{4,8},{5,9},{6,10},{7,11},{8,12},{9,13},{1... | collective-permute-start | bytes 393224 | tf_op jit(solution)/shard_map/ppermute | solution.py:52
  98.1 7.4 %collective-permute-start.32 = (f32[256,128]{1,0:T(8,128)S(1)}, f32[256,128]{1,0:T(8,128)S(1)}, u32[]{:S(2)}, u32[]{:S(2)}) collective-permute-start(f32[256,128]{1,0:T(8,128)S(1)} %get-tuple-element.167), channel_id=1, source_target_pairs={{0,12},{1,13},{2,14},{3,15},{4,0},{5,1},{6,2},{7,3},{8,4},{9,5},{1... | collective-permute-start | bytes 393224 | tf_op jit(solution)/shard_map/ppermute | solution.py:52
  105.6 15.2 %collective-permute-start.34 = (f32[256,128]{1,0:T(8,128)S(1)}, f32[256,128]{1,0:T(8,128)S(1)}, u32[]{:S(2)}, u32[]{:S(2)}) collective-permute-start(f32[256,128]{1,0:T(8,128)S(1)} %shard_map.90.refs_12_), channel_id=1, source_target_pairs={{0,34},{1,35},{2,32},{3,33},{4,38},{5,39},{6,36},{7,37},{8,42},{9,... | collective-permute-start | bytes 393224 | tf_op jit(solution)/shard_map/ppermute | solution.py:52
  110.8 12.1 %collective-permute-start.33 = (f32[256,128]{1,0:T(8,128)S(1)}, f32[256,128]{1,0:T(8,128)S(1)}, u32[]{:S(2)}, u32[]{:S(2)}) collective-permute-start(f32[256,128]{1,0:T(8,128)S(1)} %shard_map.90.refs_12_), channel_id=1, source_target_pairs={{0,32},{1,33},{2,34},{3,35},{4,36},{5,37},{6,38},{7,39},{8,40},{9,... | collective-permute-start | bytes 393224 | tf_op jit(solution)/shard_map/ppermute | solution.py:52
  123.0 7.0 %collective-permute-start.37 = (f32[128,256]{1,0:T(8,128)S(1)}, f32[128,256]{1,0:T(8,128)S(1)}, u32[]{:S(2)}, u32[]{:S(2)}) collective-permute-start(f32[128,256]{1,0:T(8,128)S(1)} %shard_map.92.refs_0_), channel_id=1, source_target_pairs={{0,4},{1,5},{2,6},{3,7},{4,8},{5,9},{6,10},{7,11},{8,12},{9,13},{1... | collective-permute-start | bytes 393224 | tf_op jit(solution)/shard_map/ppermute | solution.py:52
  124.5 8.1 %collective-permute-start.36 = (f32[128,256]{1,0:T(8,128)S(1)}, f32[128,256]{1,0:T(8,128)S(1)}, u32[]{:S(2)}, u32[]{:S(2)}) collective-permute-start(f32[128,256]{1,0:T(8,128)S(1)} %shard_map.92.refs_0_), channel_id=1, source_target_pairs={{0,8},{1,9},{2,10},{3,11},{4,12},{5,13},{6,14},{7,15},{8,0},{9,1},... | collective-permute-start | bytes 393224 | tf_op jit(solution)/shard_map/ppermute | solution.py:52
  126.7 6.0 %collective-permute-start.35 = (f32[128,256]{1,0:T(8,128)S(1)}, f32[128,256]{1,0:T(8,128)S(1)}, u32[]{:S(2)}, u32[]{:S(2)}) collective-permute-start(f32[128,256]{1,0:T(8,128)S(1)} %shard_map.92.refs_0_), channel_id=1, source_target_pairs={{0,12},{1,13},{2,14},{3,15},{4,0},{5,1},{6,2},{7,3},{8,4},{9,5},{1... | collective-permute-start | bytes 393224 | tf_op jit(solution)/shard_map/ppermute | solution.py:52
  132.8 2.0 %collective-permute-start.38 = (f32[4,128,256]{2,1,0:T(8,128)S(1)}, f32[4,128,256]{2,1,0:T(8,128)S(1)}, u32[]{:S(2)}, u32[]{:S(2)}) collective-permute-start(f32[4,128,256]{2,1,0:T(8,128)S(1)} %shard_map.93.mine), channel_id=1, source_target_pairs={{0,1},{1,0},{2,3},{3,2},{4,5},{5,4},{6,7},{7,6},{8,9},{9,8},{10,11... | collective-permute-start | bytes 1572872 | tf_op jit(solution)/shard_map/ppermute | solution.py:52
  (13 other events, 116.2 us)

commit v2 on v1

--- a/solution.py
+++ b/solution.py
@@ -86,12 +86,17 @@
 
 def prepare_kernel(pixels, scene, before, uh, ul, uth, utl, vh, vl, own):
     core, y = position()
-    for r in range(N_Y):
+
+    @pl.loop(0, N_Y)
+    def _(r):
         at = lax.rem(y + r, N_Y) * PAIR
         vh[r], vl[r] = split(scene[pl.ds(pl.multiple_of(at, PAIR), PAIR), :].T)
+
     own[...] = scene[pl.ds(pl.multiple_of(y * PAIR + core * CHUNK, CHUNK), CHUNK), :].T
-    for t in range(PIX_DEV // ROW_TILE):
-        rows = pl.ds(t * ROW_TILE, ROW_TILE)
+
+    @pl.loop(0, PIX_DEV // ROW_TILE)
+    def _(t):
+        rows = pl.ds(pl.multiple_of(t * ROW_TILE, ROW_TILE), ROW_TILE)
         value = pixels[rows, :]
         uh[rows, :], ul[rows, :] = split(value)
         uth[:, rows], utl[:, rows] = split(value.T)
@@ -226,19 +231,23 @@
     out[...] = value.T if last else value
 
 
+JOINED = (0,) + ORDER[:2]
+
+
 def join_kernel(*refs):
-    for r in range(N_Y):
-        refs[-1][r] = refs[r][...]
-
-
-def assemble_kernel(mine, other, out, sems):
+    for k in range(len(JOINED)):
+        refs[-1][k] = refs[k][...]
+
+
+def assemble_kernel(mine, other, last_mine, last_other, out, sems):
     core, y = position()
     copies = []
-    for r in range(N_Y):
-        for k, pieces in enumerate((mine, other)):
+    for k, (pieces, piece) in enumerate(((mine, last_mine), (other, last_other))):
+        for n, r in enumerate(JOINED + ORDER[2:]):
             at = lax.rem(y + r, N_Y) * PAIR + lax.rem(core + k, N_CORE) * CHUNK
             rows = pl.ds(pl.multiple_of(at, CHUNK), CHUNK)
-            copies.append(pltpu.make_async_copy(pieces.at[r], out.at[rows, :], sems.at[k, r]))
+            source = pieces.at[n] if n < len(JOINED) else piece
+            copies.append(pltpu.make_async_copy(source, out.at[rows, :], sems.at[k, n]))
     for c in copies:
         c.start()
     for c in copies:
@@ -298,14 +307,15 @@
         if not last:
             for r in ORDER:
                 other[r] = moved(mine[r], core=1)
-    joined = jax.ShapeDtypeStruct((N_Y, CHUNK, R), F32)
-    joined = call(join_kernel, joined, [VMEM] * N_Y, VMEM, [mine[r] for r in range(N_Y)])
+    joined = jax.ShapeDtypeStruct((len(JOINED), CHUNK, R), F32)
+    joined = call(join_kernel, joined, [VMEM] * len(JOINED), VMEM, [mine[r] for r in JOINED])
+    late = mine[ORDER[2]]
     scene = call(
         assemble_kernel,
         jax.ShapeDtypeStruct((ACQ_BLK, R), F32),
-        [VMEM] * 2,
+        [VMEM] * 4,
         HBM,
-        (joined, moved(joined, core=1)),
+        (joined, moved(joined, core=1), late, moved(late, core=1)),
         scratch=[pltpu.SemaphoreType.DMA((N_CORE, N_Y))],
     )
     return (pixels, scene)

time: 137 us -> 143 us (1.044)
  waiting for transfers between devices: 37.8 us -> 43.4 us
    ppermute x39 -> x40, waiting for transfers between devices: 37.8 us -> 43.4 us  [moved(): return lax.ppermute(value, BOTH, pairs)]
    ppermute x39 -> x40, starting transfers between devices: 62.4 us -> 62.2 us  [moved(): return lax.ppermute(value, BOTH, pairs)]
  transfers between devices with their start and end apart: 39 -> 40, of which waited for: 27 -> 27; matrix products, arithmetic and copies ran while one was open for 0% -> 0% of each run, Pallas kernels for 12% -> 12%
where the time goes in v2:
time: 143 us; the launch traced here: 142 us
  starting transfers between devices  62.2 us (43%)
  waiting for transfers between devices  43.4 us (30%)
  Pallas kernels  31.4 us (22%)
  local copies, waits for them, and re-layouts  3.64 us (3%)
    ppermute x40, starting transfers between devices, moved(): return lax.ppermute(value, BOTH, pairs)  62.2 us
    ppermute x40, waiting for transfers between devices, moved(): return lax.ppermute(value, BOTH, pairs)  43.4 us
    pallas_call x27, Pallas kernels, call(): pl.pallas_call(kernel, out_shape=out, in_specs=in_specs, out_specs=out_sp...  31.4 us
  transfers between devices with their start and end apart: 40, of which 27 were waited for; matrix products, arithmetic and copies ran while one was open for 0% of the time, Pallas kernels for 12%

profile of v2, /device:TPU:2, one launch (start us, length us, event | category | flops | bytes accessed | tf_op | source)
XLA Modules:
  0.0 141.7 jit_solution(8842062101969013445)
XLA Ops:
  1.4 2.3 %slice_bitcast_fusion.4 = (bf16[768,1024]{1,0:T(8,128)(2,1)S(1)}, bf16[768,1024]{1,0:T(8,128)(2,1)S(1)}) fusion(bf16[3,768,1024]{2,1,0:T(8,128)(2,1)} %param.8, bf16[3,768,1024]{2,1,0:T(8,128)(2,1)} %param.7), kind=kLoop, calls=%fused_computation.4 | loop fusion | bytes 6291456 | tf_op jit(solution)/shard_map/squeeze | solution.py:259
  8.9 3.4 %shard_map.72 = (f32[3,256,128]{2,1,0:T(8,128)S(1)}, f32[2,256,128]{2,1,0:T(8,128)S(1)}, bf16[2,768,256]{2,1,0:T(8,128)(2,1)S(1)}, bf16[2,768,256]{2,1,0:T(8,128)(2,1)S(1)}) custom-call(s32[3,1]{1,0:T(4,128)S(1)} %copy.7.occupancy, bf16[768,256]{1,0:T(8,128)(2,1)S(1)} %get-tuple-element.86.uh, bf16[768,256]{1,0:T(8,128)(2,1)S(1)} %get-tuple-element.87.ul, ...), custom_call_target="tpu_custom_call" | custom-call | flops 1207959552 | bytes 1048576 | tf_op jit(solution)/shard_map/pallas_call | solution.py:76
  12.9 3.2 %collective-permute-start.2 = (f32[256,128]{1,0:T(8,128)S(1)}, f32[256,128]{1,0:T(8,128)S(1)}, u32[]{:S(2)}, u32[]{:S(2)}) collective-permute-start(f32[256,128]{1,0:T(8,128)S(1)} %shard_map.71.refs_4_), channel_id=1, source_target_pairs={{0,8},{1,9},{2,10},{3,11},{4,12},{5,13},{6,14},{7,15},{8,0},{9,1},... | collective-permute-start | bytes 393224 | tf_op jit(solution)/shard_map/ppermute | solution.py:52
  16.9 2.6 %collective-permute-start.4 = (f32[256,128]{1,0:T(8,128)S(1)}, f32[256,128]{1,0:T(8,128)S(1)}, u32[]{:S(2)}, u32[]{:S(2)}) collective-permute-start(f32[256,128]{1,0:T(8,128)S(1)} %get-tuple-element.107), channel_id=1, source_target_pairs={{0,12},{1,13},{2,14},{3,15},{4,0},{5,1},{6,2},{7,3},{8,4},{9,5},{1... | collective-permute-start | bytes 393224 | tf_op jit(solution)/shard_map/ppermute | solution.py:52
  20.0 2.7 %collective-permute-done.3.second = f32[256,128]{1,0:T(8,128)S(1)} collective-permute-done((f32[256,128]{1,0:T(8,128)S(1)}, f32[256,128]{1,0:T(8,128)S(1)}, u32[]{:S(2)}, u32[]{:S(2)}) %collective-permute-start.3) | collective-permute-done | bytes 131104 | tf_op jit(solution)/shard_map/ppermute | solution.py:52
  23.1 7.2 %collective-permute-start.6 = (f32[256,128]{1,0:T(8,128)S(1)}, f32[256,128]{1,0:T(8,128)S(1)}, u32[]{:S(2)}, u32[]{:S(2)}) collective-permute-start(f32[256,128]{1,0:T(8,128)S(1)} %shard_map.74.refs_8_), channel_id=1, source_target_pairs={{0,242},{1,243},{2,240},{3,241},{4,246},{5,247},{6,244},{7,245},{8... | collective-permute-start | bytes 393224 | tf_op jit(solution)/shard_map/ppermute | solution.py:52
  31.8 2.0 %shard_map.75 = (f32[8,128]{1,0:T(8,128)S(1)}, f32[768,256]{1,0:T(8,128)S(1)}, bf16[768,256]{1,0:T(8,128)(2,1)S(1)}, bf16[768,256]{1,0:T(8,128)(2,1)S(1)}, bf16[...) custom-call(f32[768,256]{1,0:T(8,128)S(1)} %copy-done, bf16[1,768,256]{2,1,0:T(8,128)(2,1)S(1)} %get-tuple-element.92.refs_0_, ...), custom_call_target="tpu_custom_call" | custom-call | flops 1207959552 | bytes 1048576 | tf_op jit(solution)/shard_map/pallas_call | solution.py:76
  34.4 2.7 %collective-permute-done.5.a = f32[256,128]{1,0:T(8,128)S(1)} collective-permute-done((f32[256,128]{1,0:T(8,128)S(1)}, f32[256,128]{1,0:T(8,128)S(1)}, u32[]{:S(2)}, u32[]{:S(2)}) %collective-permute-start.5) | collective-permute-done | bytes 131104 | tf_op jit(solution)/shard_map/ppermute | solution.py:52
  37.1 3.8 %collective-permute-start.8 = (f32[256,128]{1,0:T(8,128)S(1)}, f32[256,128]{1,0:T(8,128)S(1)}, u32[]{:S(2)}, u32[]{:S(2)}) collective-permute-start(f32[256,128]{1,0:T(8,128)S(1)} %shard_map.76.refs_0_.own), channel_id=1, source_target_pairs={{0,8},{1,9},{2,10},{3,11},{4,12},{5,13},{6,14},{7,15},{8,0},{9,1},... | collective-permute-start | bytes 393224 | tf_op jit(solution)/shard_map/ppermute | solution.py:52
  41.2 3.1 %collective-permute-start.10 = (f32[256,128]{1,0:T(8,128)S(1)}, f32[256,128]{1,0:T(8,128)S(1)}, u32[]{:S(2)}, u32[]{:S(2)}) collective-permute-start(f32[256,128]{1,0:T(8,128)S(1)} %shard_map.76.refs_0_.own), channel_id=1, source_target_pairs={{0,12},{1,13},{2,14},{3,15},{4,0},{5,1},{6,2},{7,3},{8,4},{9,5},{1... | collective-permute-start | bytes 393224 | tf_op jit(solution)/shard_map/ppermute | solution.py:52
  51.6 3.5 %shard_map.80 = (f32[3,256,128]{2,1,0:T(8,128)S(1)}, f32[2,256,128]{2,1,0:T(8,128)S(1)}, bf16[2,768,256]{2,1,0:T(8,128)(2,1)S(1)}, bf16[2,768,256]{2,1,0:T(8,128...) custom-call(s32[3,1]{1,0:T(4,128)S(1)} %copy.7.occupancy, ...), custom_call_target="tpu_custom_call" | custom-call | flops 1207959552 | bytes 1048576 | tf_op jit(solution)/shard_map/pallas_call | solution.py:76
  55.3 3.6 %collective-permute-start.16 = (f32[256,128]{1,0:T(8,128)S(1)}, f32[256,128]{1,0:T(8,128)S(1)}, u32[]{:S(2)}, u32[]{:S(2)}) collective-permute-start(f32[256,128]{1,0:T(8,128)S(1)} %shard_map.79.refs_6_), channel_id=1, source_target_pairs={{0,8},{1,9},{2,10},{3,11},{4,12},{5,13},{6,14},{7,15},{8,0},{9,1},... | collective-permute-start | bytes 393224 | tf_op jit(solution)/shard_map/ppermute | solution.py:52
  59.1 3.1 %collective-permute-start.18 = (f32[256,128]{1,0:T(8,128)S(1)}, f32[256,128]{1,0:T(8,128)S(1)}, u32[]{:S(2)}, u32[]{:S(2)}) collective-permute-start(f32[256,128]{1,0:T(8,128)S(1)} %get-tuple-element.137), channel_id=1, source_target_pairs={{0,12},{1,13},{2,14},{3,15},{4,0},{5,1},{6,2},{7,3},{8,4},{9,5},{1... | collective-permute-start | bytes 393224 | tf_op jit(solution)/shard_map/ppermute | solution.py:52
  63.2 2.6 %collective-permute-done.17.second = f32[256,128]{1,0:T(8,128)S(1)} collective-permute-done((f32[256,128]{1,0:T(8,128)S(1)}, f32[256,128]{1,0:T(8,128)S(1)}, u32[]{:S(2)}, u32[]{:S(2)}) %collective-permute-start.17) | collective-permute-done | bytes 131104 | tf_op jit(solution)/shard_map/ppermute | solution.py:52
  65.8 4.4 %collective-permute-start.20 = (f32[256,128]{1,0:T(8,128)S(1)}, f32[256,128]{1,0:T(8,128)S(1)}, u32[]{:S(2)}, u32[]{:S(2)}) collective-permute-start(f32[256,128]{1,0:T(8,128)S(1)} %shard_map.82.refs_12_), channel_id=1, source_target_pairs={{0,242},{1,243},{2,240},{3,241},{4,246},{5,247},{6,244},{7,245},{8... | collective-permute-start | bytes 393224 | tf_op jit(solution)/shard_map/ppermute | solution.py:52
  71.6 2.0 %shard_map.83 = (f32[8,128]{1,0:T(8,128)S(1)}, f32[768,256]{1,0:T(8,128)S(1)}, bf16[768,256]{1,0:T(8,128)(2,1)S(1)}, bf16[768,256]{1,0:T(8,128)(2,1)S(1)}, bf16[...) custom-call(f32[768,256]{1,0:T(8,128)S(1)} %get-tuple-element.108.pixels, ...), custom_call_target="tpu_custom_call" | custom-call | flops 1207959552 | bytes 1048576 | tf_op jit(solution)/shard_map/pallas_call | solution.py:76
  73.6 2.2 %collective-permute-done.20.b = f32[256,128]{1,0:T(8,128)S(1)} collective-permute-done((f32[256,128]{1,0:T(8,128)S(1)}, f32[256,128]{1,0:T(8,128)S(1)}, u32[]{:S(2)}, u32[]{:S(2)}) %collective-permute-start.20) | collective-permute-done | bytes 131104 | tf_op jit(solution)/shard_map/ppermute | solution.py:52
  75.8 2.2 %collective-permute-done.19.a = f32[256,128]{1,0:T(8,128)S(1)} collective-permute-done((f32[256,128]{1,0:T(8,128)S(1)}, f32[256,128]{1,0:T(8,128)S(1)}, u32[]{:S(2)}, u32[]{:S(2)}) %collective-permute-start.19) | collective-permute-done | bytes 131104 | tf_op jit(solution)/shard_map/ppermute | solution.py:52
  78.0 2.4 %collective-permute-start.22 = (f32[256,128]{1,0:T(8,128)S(1)}, f32[256,128]{1,0:T(8,128)S(1)}, u32[]{:S(2)}, u32[]{:S(2)}) collective-permute-start(f32[256,128]{1,0:T(8,128)S(1)} %shard_map.84.refs_0_.own), channel_id=1, source_target_pairs={{0,8},{1,9},{2,10},{3,11},{4,12},{5,13},{6,14},{7,15},{8,0},{9,1},... | collective-permute-start | bytes 393224 | tf_op jit(solution)/shard_map/ppermute | solution.py:52
  80.7 3.2 %collective-permute-start.24 = (f32[256,128]{1,0:T(8,128)S(1)}, f32[256,128]{1,0:T(8,128)S(1)}, u32[]{:S(2)}, u32[]{:S(2)}) collective-permute-start(f32[256,128]{1,0:T(8,128)S(1)} %shard_map.84.refs_0_.own), channel_id=1, source_target_pairs={{0,12},{1,13},{2,14},{3,15},{4,0},{5,1},{6,2},{7,3},{8,4},{9,5},{1... | collective-permute-start | bytes 393224 | tf_op jit(solution)/shard_map/ppermute | solution.py:52
  83.9 2.1 %collective-permute-done.22.refs_0_ = f32[256,128]{1,0:T(8,128)S(1)} collective-permute-done((f32[256,128]{1,0:T(8,128)S(1)}, f32[256,128]{1,0:T(8,128)S(1)}, u32[]{:S(2)}, u32[]{:S(2)}) %collective-permute-start.22) | collective-permute-done | bytes 131104 | tf_op jit(solution)/shard_map/ppermute | solution.py:52
  92.2 3.4 %shard_map.88 = (f32[3,256,128]{2,1,0:T(8,128)S(1)}, f32[2,256,128]{2,1,0:T(8,128)S(1)}, bf16[2,768,256]{2,1,0:T(8,128)(2,1)S(1)}, bf16[2,768,256]{2,1,0:T(8,128...) custom-call(s32[3,1]{1,0:T(4,128)S(1)} %copy.7.occupancy, ...), custom_call_target="tpu_custom_call" | custom-call | flops 1207959552 | bytes 1048576 | tf_op jit(solution)/shard_map/pallas_call | solution.py:76
  98.5 2.3 %collective-permute-start.32 = (f32[256,128]{1,0:T(8,128)S(1)}, f32[256,128]{1,0:T(8,128)S(1)}, u32[]{:S(2)}, u32[]{:S(2)}) collective-permute-start(f32[256,128]{1,0:T(8,128)S(1)} %get-tuple-element.167), channel_id=1, source_target_pairs={{0,12},{1,13},{2,14},{3,15},{4,0},{5,1},{6,2},{7,3},{8,4},{9,5},{1... | collective-permute-start | bytes 393224 | tf_op jit(solution)/shard_map/ppermute | solution.py:52
  100.8 3.1 %collective-permute-done.30.first = f32[256,128]{1,0:T(8,128)S(1)} collective-permute-done((f32[256,128]{1,0:T(8,128)S(1)}, f32[256,128]{1,0:T(8,128)S(1)}, u32[]{:S(2)}, u32[]{:S(2)}) %collective-permute-start.30) | collective-permute-done | bytes 131104 | tf_op jit(solution)/shard_map/ppermute | solution.py:52
  106.0 5.1 %collective-permute-start.34 = (f32[256,128]{1,0:T(8,128)S(1)}, f32[256,128]{1,0:T(8,128)S(1)}, u32[]{:S(2)}, u32[]{:S(2)}) collective-permute-start(f32[256,128]{1,0:T(8,128)S(1)} %shard_map.90.refs_12_), channel_id=1, source_target_pairs={{0,34},{1,35},{2,32},{3,33},{4,38},{5,39},{6,36},{7,37},{8,42},{9,... | collective-permute-start | bytes 393224 | tf_op jit(solution)/shard_map/ppermute | solution.py:52
  111.2 2.7 %collective-permute-start.33 = (f32[256,128]{1,0:T(8,128)S(1)}, f32[256,128]{1,0:T(8,128)S(1)}, u32[]{:S(2)}, u32[]{:S(2)}) collective-permute-start(f32[256,128]{1,0:T(8,128)S(1)} %shard_map.90.refs_12_), channel_id=1, source_target_pairs={{0,32},{1,33},{2,34},{3,35},{4,36},{5,37},{6,38},{7,39},{8,40},{9,... | collective-permute-start | bytes 393224 | tf_op jit(solution)/shard_map/ppermute | solution.py:52
  113.8 2.7 %shard_map.91 = (f32[8,128]{1,0:T(8,128)S(1)}, f32[768,256]{1,0:T(8,128)}) custom-call(f32[768,256]{1,0:T(8,128)S(1)} %get-tuple-element.138.pixels, bf16[1,768,256]{2,1,0:T(8,128)(2,1)S(1)} %get-tuple-element.147.refs_0_, bf16[1,768,256]{2,1,0:T(8,128)(2,1)S(1)} %get-tuple-element.149.refs_1_, bf16[2,768,256]{2,1,0:T(8,128)(2,1)S(1)} %get-tuple-element.153.refs_2_, ...), custom_call_target="tpu_custom_call" | custom-call | flops 1207959552 | bytes 1048576 | tf_op jit(solution)/shard_map/pallas_call | solution.py:76
  116.6 4.7 %collective-permute-done.34.b = f32[256,128]{1,0:T(8,128)S(1)} collective-permute-done((f32[256,128]{1,0:T(8,128)S(1)}, f32[256,128]{1,0:T(8,128)S(1)}, u32[]{:S(2)}, u32[]{:S(2)}) %collective-permute-start.34) | collective-permute-done | bytes 131104 | tf_op jit(solution)/shard_map/ppermute | solution.py:52
  123.3 2.1 %collective-permute-start.36 = (f32[128,256]{1,0:T(8,128)S(1)}, f32[128,256]{1,0:T(8,128)S(1)}, u32[]{:S(2)}, u32[]{:S(2)}) collective-permute-start(f32[128,256]{1,0:T(8,128)S(1)} %shard_map.92.refs_0_), channel_id=1, source_target_pairs={{0,12},{1,13},{2,14},{3,15},{4,0},{5,1},{6,2},{7,3},{8,4},{9,5},{1... | collective-permute-start | bytes 393224 | tf_op jit(solution)/shard_map/ppermute | solution.py:52
  127.1 3.6 %collective-permute-done.36.refs_2_ = f32[128,256]{1,0:T(8,128)S(1)} collective-permute-done((f32[128,256]{1,0:T(8,128)S(1)}, f32[128,256]{1,0:T(8,128)S(1)}, u32[]{:S(2)}, u32[]{:S(2)}) %collective-permute-start.36) | collective-permute-done | bytes 131104 | tf_op jit(solution)/shard_map/ppermute | solution.py:52
  132.0 2.3 %collective-permute-start.38 = (f32[128,256]{1,0:T(8,128)S(1)}, f32[128,256]{1,0:T(8,128)S(1)}, u32[]{:S(2)}, u32[]{:S(2)}) collective-permute-start(f32[128,256]{1,0:T(8,128)S(1)} %shard_map.92.refs_0_), channel_id=1, source_target_pairs={{0,4},{1,5},{2,6},{3,7},{4,8},{5,9},{6,10},{7,11},{8,12},{9,13},{1... | collective-permute-start | bytes 393224 | tf_op jit(solution)/shard_map/ppermute | solution.py:52
  134.3 4.8 %collective-permute-done.38.last_mine = f32[128,256]{1,0:T(8,128)S(1)} collective-permute-done((f32[128,256]{1,0:T(8,128)S(1)}, f32[128,256]{1,0:T(8,128)S(1)}, u32[]{:S(2)}, u32[]{:S(2)}) %collective-permute-start.38) | collective-permute-done | bytes 131104 | tf_op jit(solution)/shard_map/ppermute | solution.py:52
  (95 shorter events, 39.4 us)
Async XLA Ops:
  6.8 2.1 %collective-permute-start = (f32[1,256,128]{2,1,0:T(8,128)S(1)}, f32[1,256,128]{2,1,0:T(8,128)S(1)}, u32[]{:S(2)}, u32[]{:S(2)}) collective-permute-start(f32[1,256,128]{2,1,0:T(8,128)S(1)} %get-tuple-element.97), channel_id=1, source_target_pairs={{0,1},{1,0},{2,3},{3,2},{4,5},{5,4},{6,7},{7,6},{8,9},{9,8},{10,11... | collective-permute-start | bytes 393224 | tf_op jit(solution)/shard_map/ppermute | solution.py:52
  12.3 3.8 %collective-permute-start.1 = (f32[3,256,128]{2,1,0:T(8,128)S(1)}, f32[3,256,128]{2,1,0:T(8,128)S(1)}, u32[]{:S(2)}, u32[]{:S(2)}) collective-permute-start(f32[3,256,128]{2,1,0:T(8,128)S(1)} %get-tuple-element.104), channel_id=1, source_target_pairs={{0,1},{1,0},{2,3},{3,2},{4,5},{5,4},{6,7},{7,6},{8,9},{9,8},{10,11... | collective-permute-start | bytes 1179656 | tf_op jit(solution)/shard_map/ppermute | solution.py:52
  12.9 7.1 %collective-permute-start.2 = (f32[256,128]{1,0:T(8,128)S(1)}, f32[256,128]{1,0:T(8,128)S(1)}, u32[]{:S(2)}, u32[]{:S(2)}) collective-permute-start(f32[256,128]{1,0:T(8,128)S(1)} %shard_map.71.refs_4_), channel_id=1, source_target_pairs={{0,8},{1,9},{2,10},{3,11},{4,12},{5,13},{6,14},{7,15},{8,0},{9,1},... | collective-permute-start | bytes 393224 | tf_op jit(solution)/shard_map/ppermute | solution.py:52
  16.1 6.6 %collective-permute-start.3 = (f32[256,128]{1,0:T(8,128)S(1)}, f32[256,128]{1,0:T(8,128)S(1)}, u32[]{:S(2)}, u32[]{:S(2)}) collective-permute-start(f32[256,128]{1,0:T(8,128)S(1)} %get-tuple-element.106), channel_id=1, source_target_pairs={{0,4},{1,5},{2,6},{3,7},{4,8},{5,9},{6,10},{7,11},{8,12},{9,13},{1... | collective-permute-start | bytes 393224 | tf_op jit(solution)/shard_map/ppermute | solution.py:52
  16.9 6.2 %collective-permute-start.4 = (f32[256,128]{1,0:T(8,128)S(1)}, f32[256,128]{1,0:T(8,128)S(1)}, u32[]{:S(2)}, u32[]{:S(2)}) collective-permute-start(f32[256,128]{1,0:T(8,128)S(1)} %get-tuple-element.107), channel_id=1, source_target_pairs={{0,12},{1,13},{2,14},{3,15},{4,0},{5,1},{6,2},{7,3},{8,4},{9,5},{1... | collective-permute-start | bytes 393224 | tf_op jit(solution)/shard_map/ppermute | solution.py:52
  23.1 11.3 %collective-permute-start.6 = (f32[256,128]{1,0:T(8,128)S(1)}, f32[256,128]{1,0:T(8,128)S(1)}, u32[]{:S(2)}, u32[]{:S(2)}) collective-permute-start(f32[256,128]{1,0:T(8,128)S(1)} %shard_map.74.refs_8_), channel_id=1, source_target_pairs={{0,242},{1,243},{2,240},{3,241},{4,246},{5,247},{6,244},{7,245},{8... | collective-permute-start | bytes 393224 | tf_op jit(solution)/shard_map/ppermute | solution.py:52
  30.3 6.8 %collective-permute-start.5 = (f32[256,128]{1,0:T(8,128)S(1)}, f32[256,128]{1,0:T(8,128)S(1)}, u32[]{:S(2)}, u32[]{:S(2)}) collective-permute-start(f32[256,128]{1,0:T(8,128)S(1)} %shard_map.74.refs_8_), channel_id=1, source_target_pairs={{0,240},{1,241},{2,242},{3,243},{4,244},{5,245},{6,246},{7,247},{8... | collective-permute-start | bytes 393224 | tf_op jit(solution)/shard_map/ppermute | solution.py:52
  37.1 8.1 %collective-permute-start.8 = (f32[256,128]{1,0:T(8,128)S(1)}, f32[256,128]{1,0:T(8,128)S(1)}, u32[]{:S(2)}, u32[]{:S(2)}) collective-permute-start(f32[256,128]{1,0:T(8,128)S(1)} %shard_map.76.refs_0_.own), channel_id=1, source_target_pairs={{0,8},{1,9},{2,10},{3,11},{4,12},{5,13},{6,14},{7,15},{8,0},{9,1},... | collective-permute-start | bytes 393224 | tf_op jit(solution)/shard_map/ppermute | solution.py:52
  41.0 8.9 %collective-permute-start.11 = (f32[256,128]{1,0:T(8,128)S(1)}, f32[256,128]{1,0:T(8,128)S(1)}, u32[]{:S(2)}, u32[]{:S(2)}) collective-permute-start(f32[256,128]{1,0:T(8,128)S(1)} %shard_map.76.refs_0_.own), channel_id=1, source_target_pairs={{0,4},{1,5},{2,6},{3,7},{4,8},{5,9},{6,10},{7,11},{8,12},{9,13},{1... | collective-permute-start | bytes 393224 | tf_op jit(solution)/shard_map/ppermute | solution.py:52
  41.2 9.0 %collective-permute-start.10 = (f32[256,128]{1,0:T(8,128)S(1)}, f32[256,128]{1,0:T(8,128)S(1)}, u32[]{:S(2)}, u32[]{:S(2)}) collective-permute-start(f32[256,128]{1,0:T(8,128)S(1)} %shard_map.76.refs_0_.own), channel_id=1, source_target_pairs={{0,12},{1,13},{2,14},{3,15},{4,0},{5,1},{6,2},{7,3},{8,4},{9,5},{1... | collective-permute-start | bytes 393224 | tf_op jit(solution)/shard_map/ppermute | solution.py:52
  45.2 2.4 %collective-permute-start.9 = (f32[256,128]{1,0:T(8,128)S(1)}, f32[256,128]{1,0:T(8,128)S(1)}, u32[]{:S(2)}, u32[]{:S(2)}) collective-permute-start(f32[256,128]{1,0:T(8,128)S(1)} %collective-permute-done.8.refs_0_), channel_id=1, source_target_pairs={{0,1},{1,0},{2,3},{3,2},{4,5},{5,4},{6,7},{7,6},{8,9},{9,8},{10,11... | collective-permute-start | bytes 393224 | tf_op jit(solution)/shard_map/ppermute | solution.py:52
  55.0 3.9 %collective-permute-start.15 = (f32[3,256,128]{2,1,0:T(8,128)S(1)}, f32[3,256,128]{2,1,0:T(8,128)S(1)}, u32[]{:S(2)}, u32[]{:S(2)}) collective-permute-start(f32[3,256,128]{2,1,0:T(8,128)S(1)} %get-tuple-element.134), channel_id=1, source_target_pairs={{0,1},{1,0},{2,3},{3,2},{4,5},{5,4},{6,7},{7,6},{8,9},{9,8},{10,11... | collective-permute-start | bytes 1179656 | tf_op jit(solution)/shard_map/ppermute | solution.py:52
  55.3 7.9 %collective-permute-start.16 = (f32[256,128]{1,0:T(8,128)S(1)}, f32[256,128]{1,0:T(8,128)S(1)}, u32[]{:S(2)}, u32[]{:S(2)}) collective-permute-start(f32[256,128]{1,0:T(8,128)S(1)} %shard_map.79.refs_6_), channel_id=1, source_target_pairs={{0,8},{1,9},{2,10},{3,11},{4,12},{5,13},{6,14},{7,15},{8,0},{9,1},... | collective-permute-start | bytes 393224 | tf_op jit(solution)/shard_map/ppermute | solution.py:52
  58.9 6.9 %collective-permute-start.17 = (f32[256,128]{1,0:T(8,128)S(1)}, f32[256,128]{1,0:T(8,128)S(1)}, u32[]{:S(2)}, u32[]{:S(2)}) collective-permute-start(f32[256,128]{1,0:T(8,128)S(1)} %get-tuple-element.136), channel_id=1, source_target_pairs={{0,4},{1,5},{2,6},{3,7},{4,8},{5,9},{6,10},{7,11},{8,12},{9,13},{1... | collective-permute-start | bytes 393224 | tf_op jit(solution)/shard_map/ppermute | solution.py:52
  59.1 6.7 %collective-permute-start.18 = (f32[256,128]{1,0:T(8,128)S(1)}, f32[256,128]{1,0:T(8,128)S(1)}, u32[]{:S(2)}, u32[]{:S(2)}) collective-permute-start(f32[256,128]{1,0:T(8,128)S(1)} %get-tuple-element.137), channel_id=1, source_target_pairs={{0,12},{1,13},{2,14},{3,15},{4,0},{5,1},{6,2},{7,3},{8,4},{9,5},{1... | collective-permute-start | bytes 393224 | tf_op jit(solution)/shard_map/ppermute | solution.py:52
  65.8 10.0 %collective-permute-start.20 = (f32[256,128]{1,0:T(8,128)S(1)}, f32[256,128]{1,0:T(8,128)S(1)}, u32[]{:S(2)}, u32[]{:S(2)}) collective-permute-start(f32[256,128]{1,0:T(8,128)S(1)} %shard_map.82.refs_12_), channel_id=1, source_target_pairs={{0,242},{1,243},{2,240},{3,241},{4,246},{5,247},{6,244},{7,245},{8... | collective-permute-start | bytes 393224 | tf_op jit(solution)/shard_map/ppermute | solution.py:52
  70.2 7.8 %collective-permute-start.19 = (f32[256,128]{1,0:T(8,128)S(1)}, f32[256,128]{1,0:T(8,128)S(1)}, u32[]{:S(2)}, u32[]{:S(2)}) collective-permute-start(f32[256,128]{1,0:T(8,128)S(1)} %shard_map.82.refs_12_), channel_id=1, source_target_pairs={{0,240},{1,241},{2,242},{3,243},{4,244},{5,245},{6,246},{7,247},{8... | collective-permute-start | bytes 393224 | tf_op jit(solution)/shard_map/ppermute | solution.py:52
  78.0 8.0 %collective-permute-start.22 = (f32[256,128]{1,0:T(8,128)S(1)}, f32[256,128]{1,0:T(8,128)S(1)}, u32[]{:S(2)}, u32[]{:S(2)}) collective-permute-start(f32[256,128]{1,0:T(8,128)S(1)} %shard_map.84.refs_0_.own), channel_id=1, source_target_pairs={{0,8},{1,9},{2,10},{3,11},{4,12},{5,13},{6,14},{7,15},{8,0},{9,1},... | collective-permute-start | bytes 393224 | tf_op jit(solution)/shard_map/ppermute | solution.py:52
  80.6 10.1 %collective-permute-start.25 = (f32[256,128]{1,0:T(8,128)S(1)}, f32[256,128]{1,0:T(8,128)S(1)}, u32[]{:S(2)}, u32[]{:S(2)}) collective-permute-start(f32[256,128]{1,0:T(8,128)S(1)} %shard_map.84.refs_0_.own), channel_id=1, source_target_pairs={{0,4},{1,5},{2,6},{3,7},{4,8},{5,9},{6,10},{7,11},{8,12},{9,13},{1... | collective-permute-start | bytes 393224 | tf_op jit(solution)/shard_map/ppermute | solution.py:52
  80.7 10.1 %collective-permute-start.24 = (f32[256,128]{1,0:T(8,128)S(1)}, f32[256,128]{1,0:T(8,128)S(1)}, u32[]{:S(2)}, u32[]{:S(2)}) collective-permute-start(f32[256,128]{1,0:T(8,128)S(1)} %shard_map.84.refs_0_.own), channel_id=1, source_target_pairs={{0,12},{1,13},{2,14},{3,15},{4,0},{5,1},{6,2},{7,3},{8,4},{9,5},{1... | collective-permute-start | bytes 393224 | tf_op jit(solution)/shard_map/ppermute | solution.py:52
  83.9 2.2 %collective-permute-start.21 = (f32[256,128]{1,0:T(8,128)S(1)}, f32[256,128]{1,0:T(8,128)S(1)}, u32[]{:S(2)}, u32[]{:S(2)}) collective-permute-start(f32[256,128]{1,0:T(8,128)S(1)} %shard_map.84.refs_0_.own), channel_id=1, source_target_pairs={{0,1},{1,0},{2,3},{3,2},{4,5},{5,4},{6,7},{7,6},{8,9},{9,8},{10,11... | collective-permute-start | bytes 393224 | tf_op jit(solution)/shard_map/ppermute | solution.py:52
  86.0 2.1 %collective-permute-start.23 = (f32[256,128]{1,0:T(8,128)S(1)}, f32[256,128]{1,0:T(8,128)S(1)}, u32[]{:S(2)}, u32[]{:S(2)}) collective-permute-start(f32[256,128]{1,0:T(8,128)S(1)} %collective-permute-done.22.refs_0_), channel_id=1, source_target_pairs={{0,1},{1,0},{2,3},{3,2},{4,5},{5,4},{6,7},{7,6},{8,9},{9,8},{10,11... | collective-permute-start | bytes 393224 | tf_op jit(solution)/shard_map/ppermute | solution.py:52
  95.7 1.8 %collective-permute-start.29 = (f32[3,256,128]{2,1,0:T(8,128)S(1)}, f32[3,256,128]{2,1,0:T(8,128)S(1)}, u32[]{:S(2)}, u32[]{:S(2)}) collective-permute-start(f32[3,256,128]{2,1,0:T(8,128)S(1)} %get-tuple-element.164), channel_id=1, source_target_pairs={{0,1},{1,0},{2,3},{3,2},{4,5},{5,4},{6,7},{7,6},{8,9},{9,8},{10,11... | collective-permute-start | bytes 1179656 | tf_op jit(solution)/shard_map/ppermute | solution.py:52
  96.1 7.9 %collective-permute-start.30 = (f32[256,128]{1,0:T(8,128)S(1)}, f32[256,128]{1,0:T(8,128)S(1)}, u32[]{:S(2)}, u32[]{:S(2)}) collective-permute-start(f32[256,128]{1,0:T(8,128)S(1)} %shard_map.87.refs_6_), channel_id=1, source_target_pairs={{0,8},{1,9},{2,10},{3,11},{4,12},{5,13},{6,14},{7,15},{8,0},{9,1},... | collective-permute-start | bytes 393224 | tf_op jit(solution)/shard_map/ppermute | solution.py:52
  97.5 8.5 %collective-permute-start.31 = (f32[256,128]{1,0:T(8,128)S(1)}, f32[256,128]{1,0:T(8,128)S(1)}, u32[]{:S(2)}, u32[]{:S(2)}) collective-permute-start(f32[256,128]{1,0:T(8,128)S(1)} %get-tuple-element.166), channel_id=1, source_target_pairs={{0,4},{1,5},{2,6},{3,7},{4,8},{5,9},{6,10},{7,11},{8,12},{9,13},{1... | collective-permute-start | bytes 393224 | tf_op jit(solution)/shard_map/ppermute | solution.py:52
  98.5 7.4 %collective-permute-start.32 = (f32[256,128]{1,0:T(8,128)S(1)}, f32[256,128]{1,0:T(8,128)S(1)}, u32[]{:S(2)}, u32[]{:S(2)}) collective-permute-start(f32[256,128]{1,0:T(8,128)S(1)} %get-tuple-element.167), channel_id=1, source_target_pairs={{0,12},{1,13},{2,14},{3,15},{4,0},{5,1},{6,2},{7,3},{8,4},{9,5},{1... | collective-permute-start | bytes 393224 | tf_op jit(solution)/shard_map/ppermute | solution.py:52
  106.0 15.3 %collective-permute-start.34 = (f32[256,128]{1,0:T(8,128)S(1)}, f32[256,128]{1,0:T(8,128)S(1)}, u32[]{:S(2)}, u32[]{:S(2)}) collective-permute-start(f32[256,128]{1,0:T(8,128)S(1)} %shard_map.90.refs_12_), channel_id=1, source_target_pairs={{0,34},{1,35},{2,32},{3,33},{4,38},{5,39},{6,36},{7,37},{8,42},{9,... | collective-permute-start | bytes 393224 | tf_op jit(solution)/shard_map/ppermute | solution.py:52
  111.2 12.1 %collective-permute-start.33 = (f32[256,128]{1,0:T(8,128)S(1)}, f32[256,128]{1,0:T(8,128)S(1)}, u32[]{:S(2)}, u32[]{:S(2)}) collective-permute-start(f32[256,128]{1,0:T(8,128)S(1)} %shard_map.90.refs_12_), channel_id=1, source_target_pairs={{0,32},{1,33},{2,34},{3,35},{4,36},{5,37},{6,38},{7,39},{8,40},{9,... | collective-permute-start | bytes 393224 | tf_op jit(solution)/shard_map/ppermute | solution.py:52
  123.3 7.4 %collective-permute-start.36 = (f32[128,256]{1,0:T(8,128)S(1)}, f32[128,256]{1,0:T(8,128)S(1)}, u32[]{:S(2)}, u32[]{:S(2)}) collective-permute-start(f32[128,256]{1,0:T(8,128)S(1)} %shard_map.92.refs_0_), channel_id=1, source_target_pairs={{0,12},{1,13},{2,14},{3,15},{4,0},{5,1},{6,2},{7,3},{8,4},{9,5},{1... | collective-permute-start | bytes 393224 | tf_op jit(solution)/shard_map/ppermute | solution.py:52
  125.4 6.5 %collective-permute-start.35 = (f32[128,256]{1,0:T(8,128)S(1)}, f32[128,256]{1,0:T(8,128)S(1)}, u32[]{:S(2)}, u32[]{:S(2)}) collective-permute-start(f32[128,256]{1,0:T(8,128)S(1)} %shard_map.92.refs_0_), channel_id=1, source_target_pairs={{0,8},{1,9},{2,10},{3,11},{4,12},{5,13},{6,14},{7,15},{8,0},{9,1},... | collective-permute-start | bytes 393224 | tf_op jit(solution)/shard_map/ppermute | solution.py:52
  131.9 8.6 %collective-permute-start.37 = (f32[3,128,256]{2,1,0:T(8,128)S(1)}, f32[3,128,256]{2,1,0:T(8,128)S(1)}, u32[]{:S(2)}, u32[]{:S(2)}) collective-permute-start(f32[3,128,256]{2,1,0:T(8,128)S(1)} %shard_map.93.mine), channel_id=1, source_target_pairs={{0,1},{1,0},{2,3},{3,2},{4,5},{5,4},{6,7},{7,6},{8,9},{9,8},{10,11... | collective-permute-start | bytes 1179656 | tf_op jit(solution)/shard_map/ppermute | solution.py:52
  132.0 7.1 %collective-permute-start.38 = (f32[128,256]{1,0:T(8,128)S(1)}, f32[128,256]{1,0:T(8,128)S(1)}, u32[]{:S(2)}, u32[]{:S(2)}) collective-permute-start(f32[128,256]{1,0:T(8,128)S(1)} %shard_map.92.refs_0_), channel_id=1, source_target_pairs={{0,4},{1,5},{2,6},{3,7},{4,8},{5,9},{6,10},{7,11},{8,12},{9,13},{1... | collective-permute-start | bytes 393224 | tf_op jit(solution)/shard_map/ppermute | solution.py:52
  (14 other events, 117.5 us)

commit v3 on v2

--- a/solution.py
+++ b/solution.py
@@ -124,7 +124,7 @@
     sent, kept, mh, ml = refs[-4:]
     if carried:
         sent[count] = refs[0][0]
-    flag = occupancy[step, 0].astype(F32)
+    flag = occupancy[0, step].astype(F32)
 
     def one(k, r, at):
         columns = pl.ds(pl.multiple_of(lax.rem(y + r, N_Y) * PAIR, PAIR), PAIR)
@@ -252,6 +252,10 @@
         c.start()
     for c in copies:
         c.wait()
+
+
+def per_device(pixel_factors, scene_factors, elevations, quality, occupancy):
+    return steps(pixel_factors, scene_factors, elevations, quality, occupancy.T)
 
 
 def steps(pixel_factors, scene_factors, elevations, quality, occupancy):
@@ -330,4 +334,6 @@
         P(None, ("blk", "rep")),
     )
     out_specs = (P(("blk", "rep"), None), P("blk", None))
-    return jax.shard_map(steps, mesh=mesh, in_specs=in_specs, out_specs=out_specs, check_vma=False)
+    return jax.shard_map(
+        per_device, mesh=mesh, in_specs=in_specs, out_specs=out_specs, check_vma=False
+    )

time: 143 us -> 142 us (level)
  no operation moved by 1% of the time
where the time goes in v3:
time: 142 us; the launch traced here: 141 us
  starting transfers between devices  62.2 us (44%)
  waiting for transfers between devices  43.4 us (31%)
  Pallas kernels  31.2 us (22%)
  local copies, waits for them, and re-layouts  2.89 us (2%)
    ppermute x40, starting transfers between devices, moved(): return lax.ppermute(value, BOTH, pairs)  62.2 us
    ppermute x40, waiting for transfers between devices, moved(): return lax.ppermute(value, BOTH, pairs)  43.4 us
    pallas_call x27, Pallas kernels, call(): pl.pallas_call(kernel, out_shape=out, in_specs=in_specs, out_specs=out_sp...  31.2 us
  transfers between devices with their start and end apart: 40, of which 27 were waited for; matrix products, arithmetic and copies ran while one was open for 0% of the time, Pallas kernels for 12%

profile of v3, /device:TPU:2, one launch (start us, length us, event | category | flops | bytes accessed | tf_op | source)
XLA Modules:
  0.0 140.8 jit_solution(12127663313626167983)
XLA Ops:
  0.6 2.3 %slice_bitcast_fusion.4 = (bf16[768,1024]{1,0:T(8,128)(2,1)S(1)}, bf16[768,1024]{1,0:T(8,128)(2,1)S(1)}) fusion(bf16[3,768,1024]{2,1,0:T(8,128)(2,1)} %param.8, bf16[3,768,1024]{2,1,0:T(8,128)(2,1)} %param.7), kind=kLoop, calls=%fused_computation.4 | loop fusion | bytes 6291456 | tf_op jit(solution)/shard_map/squeeze | solution.py:263
  8.2 3.3 %shard_map.72 = (f32[3,256,128]{2,1,0:T(8,128)S(1)}, f32[2,256,128]{2,1,0:T(8,128)S(1)}, bf16[2,768,256]{2,1,0:T(8,128)(2,1)S(1)}, bf16[2,768,256]{2,1,0:T(8,128)(2,1)S(1)}) custom-call(s32[1,3]{1,0:T(1,128)S(1)} %bitcast.15, bf16[768,256]{1,0:T(8,128)(2,1)S(1)} %get-tuple-element.86.uh, bf16[768,256]{1,0:T(8,128)(2,1)S(1)} %get-tuple-element.87.ul, ...), custom_call_target="tpu_custom_call" | custom-call | flops 1207959552 | bytes 1048576 | tf_op jit(solution)/shard_map/pallas_call | solution.py:76
  12.1 3.2 %collective-permute-start.2 = (f32[256,128]{1,0:T(8,128)S(1)}, f32[256,128]{1,0:T(8,128)S(1)}, u32[]{:S(2)}, u32[]{:S(2)}) collective-permute-start(f32[256,128]{1,0:T(8,128)S(1)} %shard_map.71.refs_4_), channel_id=1, source_target_pairs={{0,8},{1,9},{2,10},{3,11},{4,12},{5,13},{6,14},{7,15},{8,0},{9,1},... | collective-permute-start | bytes 393224 | tf_op jit(solution)/shard_map/ppermute | solution.py:52
  16.1 2.6 %collective-permute-start.4 = (f32[256,128]{1,0:T(8,128)S(1)}, f32[256,128]{1,0:T(8,128)S(1)}, u32[]{:S(2)}, u32[]{:S(2)}) collective-permute-start(f32[256,128]{1,0:T(8,128)S(1)} %get-tuple-element.107), channel_id=1, source_target_pairs={{0,12},{1,13},{2,14},{3,15},{4,0},{5,1},{6,2},{7,3},{8,4},{9,5},{1... | collective-permute-start | bytes 393224 | tf_op jit(solution)/shard_map/ppermute | solution.py:52
  19.2 2.7 %collective-permute-done.3.second = f32[256,128]{1,0:T(8,128)S(1)} collective-permute-done((f32[256,128]{1,0:T(8,128)S(1)}, f32[256,128]{1,0:T(8,128)S(1)}, u32[]{:S(2)}, u32[]{:S(2)}) %collective-permute-start.3) | collective-permute-done | bytes 131104 | tf_op jit(solution)/shard_map/ppermute | solution.py:52
  22.3 7.2 %collective-permute-start.6 = (f32[256,128]{1,0:T(8,128)S(1)}, f32[256,128]{1,0:T(8,128)S(1)}, u32[]{:S(2)}, u32[]{:S(2)}) collective-permute-start(f32[256,128]{1,0:T(8,128)S(1)} %shard_map.74.refs_8_), channel_id=1, source_target_pairs={{0,242},{1,243},{2,240},{3,241},{4,246},{5,247},{6,244},{7,245},{8... | collective-permute-start | bytes 393224 | tf_op jit(solution)/shard_map/ppermute | solution.py:52
  30.9 2.0 %shard_map.75 = (f32[8,128]{1,0:T(8,128)S(1)}, f32[768,256]{1,0:T(8,128)S(1)}, bf16[768,256]{1,0:T(8,128)(2,1)S(1)}, bf16[768,256]{1,0:T(8,128)(2,1)S(1)}, bf16[...) custom-call(f32[768,256]{1,0:T(8,128)S(1)} %copy-done, bf16[1,768,256]{2,1,0:T(8,128)(2,1)S(1)} %get-tuple-element.92.refs_0_, ...), custom_call_target="tpu_custom_call" | custom-call | flops 1207959552 | bytes 1048576 | tf_op jit(solution)/shard_map/pallas_call | solution.py:76
  33.6 2.7 %collective-permute-done.5.a = f32[256,128]{1,0:T(8,128)S(1)} collective-permute-done((f32[256,128]{1,0:T(8,128)S(1)}, f32[256,128]{1,0:T(8,128)S(1)}, u32[]{:S(2)}, u32[]{:S(2)}) %collective-permute-start.5) | collective-permute-done | bytes 131104 | tf_op jit(solution)/shard_map/ppermute | solution.py:52
  36.3 3.8 %collective-permute-start.8 = (f32[256,128]{1,0:T(8,128)S(1)}, f32[256,128]{1,0:T(8,128)S(1)}, u32[]{:S(2)}, u32[]{:S(2)}) collective-permute-start(f32[256,128]{1,0:T(8,128)S(1)} %shard_map.76.refs_0_.own), channel_id=1, source_target_pairs={{0,8},{1,9},{2,10},{3,11},{4,12},{5,13},{6,14},{7,15},{8,0},{9,1},... | collective-permute-start | bytes 393224 | tf_op jit(solution)/shard_map/ppermute | solution.py:52
  40.4 3.1 %collective-permute-start.10 = (f32[256,128]{1,0:T(8,128)S(1)}, f32[256,128]{1,0:T(8,128)S(1)}, u32[]{:S(2)}, u32[]{:S(2)}) collective-permute-start(f32[256,128]{1,0:T(8,128)S(1)} %shard_map.76.refs_0_.own), channel_id=1, source_target_pairs={{0,12},{1,13},{2,14},{3,15},{4,0},{5,1},{6,2},{7,3},{8,4},{9,5},{1... | collective-permute-start | bytes 393224 | tf_op jit(solution)/shard_map/ppermute | solution.py:52
  50.7 3.4 %shard_map.80 = (f32[3,256,128]{2,1,0:T(8,128)S(1)}, f32[2,256,128]{2,1,0:T(8,128)S(1)}, bf16[2,768,256]{2,1,0:T(8,128)(2,1)S(1)}, bf16[2,768,256]{2,1,0:T(8,128...) custom-call(s32[1,3]{1,0:T(1,128)S(1)} %bitcast.18, ...), custom_call_target="tpu_custom_call" | custom-call | flops 1207959552 | bytes 1048576 | tf_op jit(solution)/shard_map/pallas_call | solution.py:76
  54.5 3.6 %collective-permute-start.16 = (f32[256,128]{1,0:T(8,128)S(1)}, f32[256,128]{1,0:T(8,128)S(1)}, u32[]{:S(2)}, u32[]{:S(2)}) collective-permute-start(f32[256,128]{1,0:T(8,128)S(1)} %shard_map.79.refs_6_), channel_id=1, source_target_pairs={{0,8},{1,9},{2,10},{3,11},{4,12},{5,13},{6,14},{7,15},{8,0},{9,1},... | collective-permute-start | bytes 393224 | tf_op jit(solution)/shard_map/ppermute | solution.py:52
  58.3 3.1 %collective-permute-start.18 = (f32[256,128]{1,0:T(8,128)S(1)}, f32[256,128]{1,0:T(8,128)S(1)}, u32[]{:S(2)}, u32[]{:S(2)}) collective-permute-start(f32[256,128]{1,0:T(8,128)S(1)} %get-tuple-element.137), channel_id=1, source_target_pairs={{0,12},{1,13},{2,14},{3,15},{4,0},{5,1},{6,2},{7,3},{8,4},{9,5},{1... | collective-permute-start | bytes 393224 | tf_op jit(solution)/shard_map/ppermute | solution.py:52
  62.4 2.6 %collective-permute-done.17.second = f32[256,128]{1,0:T(8,128)S(1)} collective-permute-done((f32[256,128]{1,0:T(8,128)S(1)}, f32[256,128]{1,0:T(8,128)S(1)}, u32[]{:S(2)}, u32[]{:S(2)}) %collective-permute-start.17) | collective-permute-done | bytes 131104 | tf_op jit(solution)/shard_map/ppermute | solution.py:52
  65.0 4.4 %collective-permute-start.20 = (f32[256,128]{1,0:T(8,128)S(1)}, f32[256,128]{1,0:T(8,128)S(1)}, u32[]{:S(2)}, u32[]{:S(2)}) collective-permute-start(f32[256,128]{1,0:T(8,128)S(1)} %shard_map.82.refs_12_), channel_id=1, source_target_pairs={{0,242},{1,243},{2,240},{3,241},{4,246},{5,247},{6,244},{7,245},{8... | collective-permute-start | bytes 393224 | tf_op jit(solution)/shard_map/ppermute | solution.py:52
  70.8 2.0 %shard_map.83 = (f32[8,128]{1,0:T(8,128)S(1)}, f32[768,256]{1,0:T(8,128)S(1)}, bf16[768,256]{1,0:T(8,128)(2,1)S(1)}, bf16[768,256]{1,0:T(8,128)(2,1)S(1)}, bf16[...) custom-call(f32[768,256]{1,0:T(8,128)S(1)} %get-tuple-element.108.pixels, ...), custom_call_target="tpu_custom_call" | custom-call | flops 1207959552 | bytes 1048576 | tf_op jit(solution)/shard_map/pallas_call | solution.py:76
  72.8 2.2 %collective-permute-done.20.b = f32[256,128]{1,0:T(8,128)S(1)} collective-permute-done((f32[256,128]{1,0:T(8,128)S(1)}, f32[256,128]{1,0:T(8,128)S(1)}, u32[]{:S(2)}, u32[]{:S(2)}) %collective-permute-start.20) | collective-permute-done | bytes 131104 | tf_op jit(solution)/shard_map/ppermute | solution.py:52
  75.0 2.2 %collective-permute-done.19.a = f32[256,128]{1,0:T(8,128)S(1)} collective-permute-done((f32[256,128]{1,0:T(8,128)S(1)}, f32[256,128]{1,0:T(8,128)S(1)}, u32[]{:S(2)}, u32[]{:S(2)}) %collective-permute-start.19) | collective-permute-done | bytes 131104 | tf_op jit(solution)/shard_map/ppermute | solution.py:52
  77.2 2.4 %collective-permute-start.22 = (f32[256,128]{1,0:T(8,128)S(1)}, f32[256,128]{1,0:T(8,128)S(1)}, u32[]{:S(2)}, u32[]{:S(2)}) collective-permute-start(f32[256,128]{1,0:T(8,128)S(1)} %shard_map.84.refs_0_.own), channel_id=1, source_target_pairs={{0,8},{1,9},{2,10},{3,11},{4,12},{5,13},{6,14},{7,15},{8,0},{9,1},... | collective-permute-start | bytes 393224 | tf_op jit(solution)/shard_map/ppermute | solution.py:52
  79.8 3.2 %collective-permute-start.24 = (f32[256,128]{1,0:T(8,128)S(1)}, f32[256,128]{1,0:T(8,128)S(1)}, u32[]{:S(2)}, u32[]{:S(2)}) collective-permute-start(f32[256,128]{1,0:T(8,128)S(1)} %shard_map.84.refs_0_.own), channel_id=1, source_target_pairs={{0,12},{1,13},{2,14},{3,15},{4,0},{5,1},{6,2},{7,3},{8,4},{9,5},{1... | collective-permute-start | bytes 393224 | tf_op jit(solution)/shard_map/ppermute | solution.py:52
  83.0 2.1 %collective-permute-done.22.refs_0_ = f32[256,128]{1,0:T(8,128)S(1)} collective-permute-done((f32[256,128]{1,0:T(8,128)S(1)}, f32[256,128]{1,0:T(8,128)S(1)}, u32[]{:S(2)}, u32[]{:S(2)}) %collective-permute-start.22) | collective-permute-done | bytes 131104 | tf_op jit(solution)/shard_map/ppermute | solution.py:52
  91.3 3.4 %shard_map.88 = (f32[3,256,128]{2,1,0:T(8,128)S(1)}, f32[2,256,128]{2,1,0:T(8,128)S(1)}, bf16[2,768,256]{2,1,0:T(8,128)(2,1)S(1)}, bf16[2,768,256]{2,1,0:T(8,128...) custom-call(s32[1,3]{1,0:T(1,128)S(1)} %bitcast.21, ...), custom_call_target="tpu_custom_call" | custom-call | flops 1207959552 | bytes 1048576 | tf_op jit(solution)/shard_map/pallas_call | solution.py:76
  97.7 2.3 %collective-permute-start.32 = (f32[256,128]{1,0:T(8,128)S(1)}, f32[256,128]{1,0:T(8,128)S(1)}, u32[]{:S(2)}, u32[]{:S(2)}) collective-permute-start(f32[256,128]{1,0:T(8,128)S(1)} %get-tuple-element.167), channel_id=1, source_target_pairs={{0,12},{1,13},{2,14},{3,15},{4,0},{5,1},{6,2},{7,3},{8,4},{9,5},{1... | collective-permute-start | bytes 393224 | tf_op jit(solution)/shard_map/ppermute | solution.py:52
  100.0 3.1 %collective-permute-done.30.first = f32[256,128]{1,0:T(8,128)S(1)} collective-permute-done((f32[256,128]{1,0:T(8,128)S(1)}, f32[256,128]{1,0:T(8,128)S(1)}, u32[]{:S(2)}, u32[]{:S(2)}) %collective-permute-start.30) | collective-permute-done | bytes 131104 | tf_op jit(solution)/shard_map/ppermute | solution.py:52
  105.2 5.1 %collective-permute-start.34 = (f32[256,128]{1,0:T(8,128)S(1)}, f32[256,128]{1,0:T(8,128)S(1)}, u32[]{:S(2)}, u32[]{:S(2)}) collective-permute-start(f32[256,128]{1,0:T(8,128)S(1)} %shard_map.90.refs_12_), channel_id=1, source_target_pairs={{0,34},{1,35},{2,32},{3,33},{4,38},{5,39},{6,36},{7,37},{8,42},{9,... | collective-permute-start | bytes 393224 | tf_op jit(solution)/shard_map/ppermute | solution.py:52
  110.3 2.7 %collective-permute-start.33 = (f32[256,128]{1,0:T(8,128)S(1)}, f32[256,128]{1,0:T(8,128)S(1)}, u32[]{:S(2)}, u32[]{:S(2)}) collective-permute-start(f32[256,128]{1,0:T(8,128)S(1)} %shard_map.90.refs_12_), channel_id=1, source_target_pairs={{0,32},{1,33},{2,34},{3,35},{4,36},{5,37},{6,38},{7,39},{8,40},{9,... | collective-permute-start | bytes 393224 | tf_op jit(solution)/shard_map/ppermute | solution.py:52
  113.0 2.7 %shard_map.91 = (f32[8,128]{1,0:T(8,128)S(1)}, f32[768,256]{1,0:T(8,128)}) custom-call(f32[768,256]{1,0:T(8,128)S(1)} %get-tuple-element.138.pixels, bf16[1,768,256]{2,1,0:T(8,128)(2,1)S(1)} %get-tuple-element.147.refs_0_, bf16[1,768,256]{2,1,0:T(8,128)(2,1)S(1)} %get-tuple-element.149.refs_1_, bf16[2,768,256]{2,1,0:T(8,128)(2,1)S(1)} %get-tuple-element.153.refs_2_, ...), custom_call_target="tpu_custom_call" | custom-call | flops 1207959552 | bytes 1048576 | tf_op jit(solution)/shard_map/pallas_call | solution.py:76
  115.7 4.7 %collective-permute-done.34.b = f32[256,128]{1,0:T(8,128)S(1)} collective-permute-done((f32[256,128]{1,0:T(8,128)S(1)}, f32[256,128]{1,0:T(8,128)S(1)}, u32[]{:S(2)}, u32[]{:S(2)}) %collective-permute-start.34) | collective-permute-done | bytes 131104 | tf_op jit(solution)/shard_map/ppermute | solution.py:52
  122.5 2.1 %collective-permute-start.36 = (f32[128,256]{1,0:T(8,128)S(1)}, f32[128,256]{1,0:T(8,128)S(1)}, u32[]{:S(2)}, u32[]{:S(2)}) collective-permute-start(f32[128,256]{1,0:T(8,128)S(1)} %shard_map.92.refs_0_), channel_id=1, source_target_pairs={{0,12},{1,13},{2,14},{3,15},{4,0},{5,1},{6,2},{7,3},{8,4},{9,5},{1... | collective-permute-start | bytes 393224 | tf_op jit(solution)/shard_map/ppermute | solution.py:52
  126.3 3.6 %collective-permute-done.36.refs_2_ = f32[128,256]{1,0:T(8,128)S(1)} collective-permute-done((f32[128,256]{1,0:T(8,128)S(1)}, f32[128,256]{1,0:T(8,128)S(1)}, u32[]{:S(2)}, u32[]{:S(2)}) %collective-permute-start.36) | collective-permute-done | bytes 131104 | tf_op jit(solution)/shard_map/ppermute | solution.py:52
  131.2 2.3 %collective-permute-start.38 = (f32[128,256]{1,0:T(8,128)S(1)}, f32[128,256]{1,0:T(8,128)S(1)}, u32[]{:S(2)}, u32[]{:S(2)}) collective-permute-start(f32[128,256]{1,0:T(8,128)S(1)} %shard_map.92.refs_0_), channel_id=1, source_target_pairs={{0,4},{1,5},{2,6},{3,7},{4,8},{5,9},{6,10},{7,11},{8,12},{9,13},{1... | collective-permute-start | bytes 393224 | tf_op jit(solution)/shard_map/ppermute | solution.py:52
  133.4 4.8 %collective-permute-done.38.last_mine = f32[128,256]{1,0:T(8,128)S(1)} collective-permute-done((f32[128,256]{1,0:T(8,128)S(1)}, f32[128,256]{1,0:T(8,128)S(1)}, u32[]{:S(2)}, u32[]{:S(2)}) %collective-permute-start.38) | collective-permute-done | bytes 131104 | tf_op jit(solution)/shard_map/ppermute | solution.py:52
  (96 shorter events, 38.5 us)
Async XLA Ops:
  6.1 2.1 %collective-permute-start = (f32[1,256,128]{2,1,0:T(8,128)S(1)}, f32[1,256,128]{2,1,0:T(8,128)S(1)}, u32[]{:S(2)}, u32[]{:S(2)}) collective-permute-start(f32[1,256,128]{2,1,0:T(8,128)S(1)} %get-tuple-element.97), channel_id=1, source_target_pairs={{0,1},{1,0},{2,3},{3,2},{4,5},{5,4},{6,7},{7,6},{8,9},{9,8},{10,11... | collective-permute-start | bytes 393224 | tf_op jit(solution)/shard_map/ppermute | solution.py:52
  11.5 3.8 %collective-permute-start.1 = (f32[3,256,128]{2,1,0:T(8,128)S(1)}, f32[3,256,128]{2,1,0:T(8,128)S(1)}, u32[]{:S(2)}, u32[]{:S(2)}) collective-permute-start(f32[3,256,128]{2,1,0:T(8,128)S(1)} %get-tuple-element.104), channel_id=1, source_target_pairs={{0,1},{1,0},{2,3},{3,2},{4,5},{5,4},{6,7},{7,6},{8,9},{9,8},{10,11... | collective-permute-start | bytes 1179656 | tf_op jit(solution)/shard_map/ppermute | solution.py:52
  12.1 7.1 %collective-permute-start.2 = (f32[256,128]{1,0:T(8,128)S(1)}, f32[256,128]{1,0:T(8,128)S(1)}, u32[]{:S(2)}, u32[]{:S(2)}) collective-permute-start(f32[256,128]{1,0:T(8,128)S(1)} %shard_map.71.refs_4_), channel_id=1, source_target_pairs={{0,8},{1,9},{2,10},{3,11},{4,12},{5,13},{6,14},{7,15},{8,0},{9,1},... | collective-permute-start | bytes 393224 | tf_op jit(solution)/shard_map/ppermute | solution.py:52
  15.3 6.6 %collective-permute-start.3 = (f32[256,128]{1,0:T(8,128)S(1)}, f32[256,128]{1,0:T(8,128)S(1)}, u32[]{:S(2)}, u32[]{:S(2)}) collective-permute-start(f32[256,128]{1,0:T(8,128)S(1)} %get-tuple-element.106), channel_id=1, source_target_pairs={{0,4},{1,5},{2,6},{3,7},{4,8},{5,9},{6,10},{7,11},{8,12},{9,13},{1... | collective-permute-start | bytes 393224 | tf_op jit(solution)/shard_map/ppermute | solution.py:52
  16.1 6.2 %collective-permute-start.4 = (f32[256,128]{1,0:T(8,128)S(1)}, f32[256,128]{1,0:T(8,128)S(1)}, u32[]{:S(2)}, u32[]{:S(2)}) collective-permute-start(f32[256,128]{1,0:T(8,128)S(1)} %get-tuple-element.107), channel_id=1, source_target_pairs={{0,12},{1,13},{2,14},{3,15},{4,0},{5,1},{6,2},{7,3},{8,4},{9,5},{1... | collective-permute-start | bytes 393224 | tf_op jit(solution)/shard_map/ppermute | solution.py:52
  22.3 11.3 %collective-permute-start.6 = (f32[256,128]{1,0:T(8,128)S(1)}, f32[256,128]{1,0:T(8,128)S(1)}, u32[]{:S(2)}, u32[]{:S(2)}) collective-permute-start(f32[256,128]{1,0:T(8,128)S(1)} %shard_map.74.refs_8_), channel_id=1, source_target_pairs={{0,242},{1,243},{2,240},{3,241},{4,246},{5,247},{6,244},{7,245},{8... | collective-permute-start | bytes 393224 | tf_op jit(solution)/shard_map/ppermute | solution.py:52
  29.5 6.8 %collective-permute-start.5 = (f32[256,128]{1,0:T(8,128)S(1)}, f32[256,128]{1,0:T(8,128)S(1)}, u32[]{:S(2)}, u32[]{:S(2)}) collective-permute-start(f32[256,128]{1,0:T(8,128)S(1)} %shard_map.74.refs_8_), channel_id=1, source_target_pairs={{0,240},{1,241},{2,242},{3,243},{4,244},{5,245},{6,246},{7,247},{8... | collective-permute-start | bytes 393224 | tf_op jit(solution)/shard_map/ppermute | solution.py:52
  36.3 8.1 %collective-permute-start.8 = (f32[256,128]{1,0:T(8,128)S(1)}, f32[256,128]{1,0:T(8,128)S(1)}, u32[]{:S(2)}, u32[]{:S(2)}) collective-permute-start(f32[256,128]{1,0:T(8,128)S(1)} %shard_map.76.refs_0_.own), channel_id=1, source_target_pairs={{0,8},{1,9},{2,10},{3,11},{4,12},{5,13},{6,14},{7,15},{8,0},{9,1},... | collective-permute-start | bytes 393224 | tf_op jit(solution)/shard_map/ppermute | solution.py:52
  40.2 8.9 %collective-permute-start.11 = (f32[256,128]{1,0:T(8,128)S(1)}, f32[256,128]{1,0:T(8,128)S(1)}, u32[]{:S(2)}, u32[]{:S(2)}) collective-permute-start(f32[256,128]{1,0:T(8,128)S(1)} %shard_map.76.refs_0_.own), channel_id=1, source_target_pairs={{0,4},{1,5},{2,6},{3,7},{4,8},{5,9},{6,10},{7,11},{8,12},{9,13},{1... | collective-permute-start | bytes 393224 | tf_op jit(solution)/shard_map/ppermute | solution.py:52
  40.4 8.9 %collective-permute-start.10 = (f32[256,128]{1,0:T(8,128)S(1)}, f32[256,128]{1,0:T(8,128)S(1)}, u32[]{:S(2)}, u32[]{:S(2)}) collective-permute-start(f32[256,128]{1,0:T(8,128)S(1)} %shard_map.76.refs_0_.own), channel_id=1, source_target_pairs={{0,12},{1,13},{2,14},{3,15},{4,0},{5,1},{6,2},{7,3},{8,4},{9,5},{1... | collective-permute-start | bytes 393224 | tf_op jit(solution)/shard_map/ppermute | solution.py:52
  44.4 2.4 %collective-permute-start.9 = (f32[256,128]{1,0:T(8,128)S(1)}, f32[256,128]{1,0:T(8,128)S(1)}, u32[]{:S(2)}, u32[]{:S(2)}) collective-permute-start(f32[256,128]{1,0:T(8,128)S(1)} %collective-permute-done.8.refs_0_), channel_id=1, source_target_pairs={{0,1},{1,0},{2,3},{3,2},{4,5},{5,4},{6,7},{7,6},{8,9},{9,8},{10,11... | collective-permute-start | bytes 393224 | tf_op jit(solution)/shard_map/ppermute | solution.py:52
  54.2 3.9 %collective-permute-start.15 = (f32[3,256,128]{2,1,0:T(8,128)S(1)}, f32[3,256,128]{2,1,0:T(8,128)S(1)}, u32[]{:S(2)}, u32[]{:S(2)}) collective-permute-start(f32[3,256,128]{2,1,0:T(8,128)S(1)} %get-tuple-element.134), channel_id=1, source_target_pairs={{0,1},{1,0},{2,3},{3,2},{4,5},{5,4},{6,7},{7,6},{8,9},{9,8},{10,11... | collective-permute-start | bytes 1179656 | tf_op jit(solution)/shard_map/ppermute | solution.py:52
  54.5 7.9 %collective-permute-start.16 = (f32[256,128]{1,0:T(8,128)S(1)}, f32[256,128]{1,0:T(8,128)S(1)}, u32[]{:S(2)}, u32[]{:S(2)}) collective-permute-start(f32[256,128]{1,0:T(8,128)S(1)} %shard_map.79.refs_6_), channel_id=1, source_target_pairs={{0,8},{1,9},{2,10},{3,11},{4,12},{5,13},{6,14},{7,15},{8,0},{9,1},... | collective-permute-start | bytes 393224 | tf_op jit(solution)/shard_map/ppermute | solution.py:52
  58.1 6.8 %collective-permute-start.17 = (f32[256,128]{1,0:T(8,128)S(1)}, f32[256,128]{1,0:T(8,128)S(1)}, u32[]{:S(2)}, u32[]{:S(2)}) collective-permute-start(f32[256,128]{1,0:T(8,128)S(1)} %get-tuple-element.136), channel_id=1, source_target_pairs={{0,4},{1,5},{2,6},{3,7},{4,8},{5,9},{6,10},{7,11},{8,12},{9,13},{1... | collective-permute-start | bytes 393224 | tf_op jit(solution)/shard_map/ppermute | solution.py:52
  58.3 6.7 %collective-permute-start.18 = (f32[256,128]{1,0:T(8,128)S(1)}, f32[256,128]{1,0:T(8,128)S(1)}, u32[]{:S(2)}, u32[]{:S(2)}) collective-permute-start(f32[256,128]{1,0:T(8,128)S(1)} %get-tuple-element.137), channel_id=1, source_target_pairs={{0,12},{1,13},{2,14},{3,15},{4,0},{5,1},{6,2},{7,3},{8,4},{9,5},{1... | collective-permute-start | bytes 393224 | tf_op jit(solution)/shard_map/ppermute | solution.py:52
  65.0 10.0 %collective-permute-start.20 = (f32[256,128]{1,0:T(8,128)S(1)}, f32[256,128]{1,0:T(8,128)S(1)}, u32[]{:S(2)}, u32[]{:S(2)}) collective-permute-start(f32[256,128]{1,0:T(8,128)S(1)} %shard_map.82.refs_12_), channel_id=1, source_target_pairs={{0,242},{1,243},{2,240},{3,241},{4,246},{5,247},{6,244},{7,245},{8... | collective-permute-start | bytes 393224 | tf_op jit(solution)/shard_map/ppermute | solution.py:52
  69.4 7.8 %collective-permute-start.19 = (f32[256,128]{1,0:T(8,128)S(1)}, f32[256,128]{1,0:T(8,128)S(1)}, u32[]{:S(2)}, u32[]{:S(2)}) collective-permute-start(f32[256,128]{1,0:T(8,128)S(1)} %shard_map.82.refs_12_), channel_id=1, source_target_pairs={{0,240},{1,241},{2,242},{3,243},{4,244},{5,245},{6,246},{7,247},{8... | collective-permute-start | bytes 393224 | tf_op jit(solution)/shard_map/ppermute | solution.py:52
  77.2 8.0 %collective-permute-start.22 = (f32[256,128]{1,0:T(8,128)S(1)}, f32[256,128]{1,0:T(8,128)S(1)}, u32[]{:S(2)}, u32[]{:S(2)}) collective-permute-start(f32[256,128]{1,0:T(8,128)S(1)} %shard_map.84.refs_0_.own), channel_id=1, source_target_pairs={{0,8},{1,9},{2,10},{3,11},{4,12},{5,13},{6,14},{7,15},{8,0},{9,1},... | collective-permute-start | bytes 393224 | tf_op jit(solution)/shard_map/ppermute | solution.py:52
  79.7 10.1 %collective-permute-start.25 = (f32[256,128]{1,0:T(8,128)S(1)}, f32[256,128]{1,0:T(8,128)S(1)}, u32[]{:S(2)}, u32[]{:S(2)}) collective-permute-start(f32[256,128]{1,0:T(8,128)S(1)} %shard_map.84.refs_0_.own), channel_id=1, source_target_pairs={{0,4},{1,5},{2,6},{3,7},{4,8},{5,9},{6,10},{7,11},{8,12},{9,13},{1... | collective-permute-start | bytes 393224 | tf_op jit(solution)/shard_map/ppermute | solution.py:52
  79.8 10.1 %collective-permute-start.24 = (f32[256,128]{1,0:T(8,128)S(1)}, f32[256,128]{1,0:T(8,128)S(1)}, u32[]{:S(2)}, u32[]{:S(2)}) collective-permute-start(f32[256,128]{1,0:T(8,128)S(1)} %shard_map.84.refs_0_.own), channel_id=1, source_target_pairs={{0,12},{1,13},{2,14},{3,15},{4,0},{5,1},{6,2},{7,3},{8,4},{9,5},{1... | collective-permute-start | bytes 393224 | tf_op jit(solution)/shard_map/ppermute | solution.py:52
  83.0 2.2 %collective-permute-start.21 = (f32[256,128]{1,0:T(8,128)S(1)}, f32[256,128]{1,0:T(8,128)S(1)}, u32[]{:S(2)}, u32[]{:S(2)}) collective-permute-start(f32[256,128]{1,0:T(8,128)S(1)} %shard_map.84.refs_0_.own), channel_id=1, source_target_pairs={{0,1},{1,0},{2,3},{3,2},{4,5},{5,4},{6,7},{7,6},{8,9},{9,8},{10,11... | collective-permute-start | bytes 393224 | tf_op jit(solution)/shard_map/ppermute | solution.py:52
  85.1 2.1 %collective-permute-start.23 = (f32[256,128]{1,0:T(8,128)S(1)}, f32[256,128]{1,0:T(8,128)S(1)}, u32[]{:S(2)}, u32[]{:S(2)}) collective-permute-start(f32[256,128]{1,0:T(8,128)S(1)} %collective-permute-done.22.refs_0_), channel_id=1, source_target_pairs={{0,1},{1,0},{2,3},{3,2},{4,5},{5,4},{6,7},{7,6},{8,9},{9,8},{10,11... | collective-permute-start | bytes 393224 | tf_op jit(solution)/shard_map/ppermute | solution.py:52
  94.8 1.8 %collective-permute-start.29 = (f32[3,256,128]{2,1,0:T(8,128)S(1)}, f32[3,256,128]{2,1,0:T(8,128)S(1)}, u32[]{:S(2)}, u32[]{:S(2)}) collective-permute-start(f32[3,256,128]{2,1,0:T(8,128)S(1)} %get-tuple-element.164), channel_id=1, source_target_pairs={{0,1},{1,0},{2,3},{3,2},{4,5},{5,4},{6,7},{7,6},{8,9},{9,8},{10,11... | collective-permute-start | bytes 1179656 | tf_op jit(solution)/shard_map/ppermute | solution.py:52
  95.2 7.9 %collective-permute-start.30 = (f32[256,128]{1,0:T(8,128)S(1)}, f32[256,128]{1,0:T(8,128)S(1)}, u32[]{:S(2)}, u32[]{:S(2)}) collective-permute-start(f32[256,128]{1,0:T(8,128)S(1)} %shard_map.87.refs_6_), channel_id=1, source_target_pairs={{0,8},{1,9},{2,10},{3,11},{4,12},{5,13},{6,14},{7,15},{8,0},{9,1},... | collective-permute-start | bytes 393224 | tf_op jit(solution)/shard_map/ppermute | solution.py:52
  96.7 8.5 %collective-permute-start.31 = (f32[256,128]{1,0:T(8,128)S(1)}, f32[256,128]{1,0:T(8,128)S(1)}, u32[]{:S(2)}, u32[]{:S(2)}) collective-permute-start(f32[256,128]{1,0:T(8,128)S(1)} %get-tuple-element.166), channel_id=1, source_target_pairs={{0,4},{1,5},{2,6},{3,7},{4,8},{5,9},{6,10},{7,11},{8,12},{9,13},{1... | collective-permute-start | bytes 393224 | tf_op jit(solution)/shard_map/ppermute | solution.py:52
  97.7 7.5 %collective-permute-start.32 = (f32[256,128]{1,0:T(8,128)S(1)}, f32[256,128]{1,0:T(8,128)S(1)}, u32[]{:S(2)}, u32[]{:S(2)}) collective-permute-start(f32[256,128]{1,0:T(8,128)S(1)} %get-tuple-element.167), channel_id=1, source_target_pairs={{0,12},{1,13},{2,14},{3,15},{4,0},{5,1},{6,2},{7,3},{8,4},{9,5},{1... | collective-permute-start | bytes 393224 | tf_op jit(solution)/shard_map/ppermute | solution.py:52
  105.2 15.3 %collective-permute-start.34 = (f32[256,128]{1,0:T(8,128)S(1)}, f32[256,128]{1,0:T(8,128)S(1)}, u32[]{:S(2)}, u32[]{:S(2)}) collective-permute-start(f32[256,128]{1,0:T(8,128)S(1)} %shard_map.90.refs_12_), channel_id=1, source_target_pairs={{0,34},{1,35},{2,32},{3,33},{4,38},{5,39},{6,36},{7,37},{8,42},{9,... | collective-permute-start | bytes 393224 | tf_op jit(solution)/shard_map/ppermute | solution.py:52
  110.3 12.1 %collective-permute-start.33 = (f32[256,128]{1,0:T(8,128)S(1)}, f32[256,128]{1,0:T(8,128)S(1)}, u32[]{:S(2)}, u32[]{:S(2)}) collective-permute-start(f32[256,128]{1,0:T(8,128)S(1)} %shard_map.90.refs_12_), channel_id=1, source_target_pairs={{0,32},{1,33},{2,34},{3,35},{4,36},{5,37},{6,38},{7,39},{8,40},{9,... | collective-permute-start | bytes 393224 | tf_op jit(solution)/shard_map/ppermute | solution.py:52
  122.5 7.4 %collective-permute-start.36 = (f32[128,256]{1,0:T(8,128)S(1)}, f32[128,256]{1,0:T(8,128)S(1)}, u32[]{:S(2)}, u32[]{:S(2)}) collective-permute-start(f32[128,256]{1,0:T(8,128)S(1)} %shard_map.92.refs_0_), channel_id=1, source_target_pairs={{0,12},{1,13},{2,14},{3,15},{4,0},{5,1},{6,2},{7,3},{8,4},{9,5},{1... | collective-permute-start | bytes 393224 | tf_op jit(solution)/shard_map/ppermute | solution.py:52
  124.6 6.5 %collective-permute-start.35 = (f32[128,256]{1,0:T(8,128)S(1)}, f32[128,256]{1,0:T(8,128)S(1)}, u32[]{:S(2)}, u32[]{:S(2)}) collective-permute-start(f32[128,256]{1,0:T(8,128)S(1)} %shard_map.92.refs_0_), channel_id=1, source_target_pairs={{0,8},{1,9},{2,10},{3,11},{4,12},{5,13},{6,14},{7,15},{8,0},{9,1},... | collective-permute-start | bytes 393224 | tf_op jit(solution)/shard_map/ppermute | solution.py:52
  131.1 8.6 %collective-permute-start.37 = (f32[3,128,256]{2,1,0:T(8,128)S(1)}, f32[3,128,256]{2,1,0:T(8,128)S(1)}, u32[]{:S(2)}, u32[]{:S(2)}) collective-permute-start(f32[3,128,256]{2,1,0:T(8,128)S(1)} %shard_map.93.mine), channel_id=1, source_target_pairs={{0,1},{1,0},{2,3},{3,2},{4,5},{5,4},{6,7},{7,6},{8,9},{9,8},{10,11... | collective-permute-start | bytes 1179656 | tf_op jit(solution)/shard_map/ppermute | solution.py:52
  131.2 7.1 %collective-permute-start.38 = (f32[128,256]{1,0:T(8,128)S(1)}, f32[128,256]{1,0:T(8,128)S(1)}, u32[]{:S(2)}, u32[]{:S(2)}) collective-permute-start(f32[128,256]{1,0:T(8,128)S(1)} %shard_map.92.refs_0_), channel_id=1, source_target_pairs={{0,4},{1,5},{2,6},{3,7},{4,8},{5,9},{6,10},{7,11},{8,12},{9,13},{1... | collective-permute-start | bytes 393224 | tf_op jit(solution)/shard_map/ppermute | solution.py:52
  (15 other events, 118.5 us)
